TPU v7x, 512 devices: a whole 4x8x8 slice. The times are simulated.
512 devices in a mesh: req: 16 (over z, core), seq: 32 (over y, x).
Axes of the slice: x: 4, y: 8, z: 8, core: 2. Of those that a mesh axis runs over, the one named last changes fastest.
Arguments:
- queries: bfloat16 [16, 128, 4096], P('req', 'seq'), may hold values from -160 to 160
- kv_cache: bfloat16 [16, 16384, 2, 256], P('req', 'seq'), may hold values from -6 to 6
- tree_kv: bfloat16 [16, 128, 2, 256], P('req', 'seq'), may hold values from -14 to 14
- context_lengths: int32 [16], P('req'), may hold values from 2048 to 16384, as said below
- tree_parents: int32 [16, 128], P('req'), may hold values from -1 to 126, as said below
- resid: bfloat16 [16, 128, 4096], P('req', 'seq'), may hold values from -6 to 6
- out_weight: bfloat16 [4096, 4096], P('seq'), may hold values from -0.5 to 0.5
- norm_gain: bfloat16 [4096], replicated, may hold values from 0.099609375 to 1.8984375
- expert_ids: int32 [16, 128, 8], P('req'), may hold values from 0 to 63, all different within a row; in each aligned block of 128 rows (0 to 127, 128 to 255, ..., all dimensions but the last counted through in order) at most 32 rows name the same one
- gate_weights: bfloat16 [16, 128, 8], P('req'), may hold values from 0.049804688 to 0.5
- w_gate: bfloat16 [512, 4096, 128], P(('req', 'seq')), may hold values from -0.09375 to 0.09375
- w_up: bfloat16 [512, 4096, 128], P(('req', 'seq')), may hold values from -0.09375 to 0.09375
- w_down: bfloat16 [512, 128, 4096], P(('req', 'seq')), may hold values from -0.375 to 0.375
Outputs:
- attended: bfloat16 [16, 128, 4096], P('req', 'seq')
- expert_sum: bfloat16 [16, 128, 4096], P('req', 'seq')
Inputs may be any that keep to these rules, and one draw needn't show every extreme that they name: `expert_ids`: each row names 8 different experts; among the rows of one request no expert is named by more than 32 rows. `tree_parents`: each request holds 4 trees of 32 nodes in a row; a tree's first node has parent -1, every other node's parent is an earlier node of the same tree; the request's last node has parent 128 - 2. `context_lengths`: at least one request uses all 16384 positions.
All inputs are finite; a program needn't handle non-finite values.
Results may differ from a plain program's by a relative error of at most 0.01615.
Values may be sent and summed in bfloat16 or wider, within the bound.
A program may use at most 64 MiB of HBM per device.

v0:
```python
import jax
import jax.numpy as jnp
from jax import lax
from jax.sharding import PartitionSpec as P

DH = 128
HQ = 32
KVH = 2
EXPERTS = 64
CAP = 32
SPLIT = 8


NEG = -1e30
EPS = 1e-06


def ancestry(parents):
    count = parents.shape[0]
    node = jnp.arange(count, dtype=jnp.int32)
    linked = (parents[:, None] == node[None, :]) | (node[:, None] == node[None, :])
    reach = linked.astype(jnp.bfloat16)
    hops = 1
    while hops < count:
        paths = jnp.dot(reach, reach, preferred_element_type=jnp.float32)
        reach = jnp.minimum(paths, 1.0).astype(jnp.bfloat16)
        hops = hops * 2
    return reach > 0.5


def shard_partial(query, block, length, first):
    rows = query.shape[0]
    group = HQ // KVH
    span = block.shape[0]
    keys = block[:, 0].reshape(span, KVH, DH)
    values = block[:, 1].reshape(span, KVH, DH)
    heads = query.reshape(rows, KVH, group, DH)
    scores = jnp.einsum("rkgd,tkd->rkgt", heads, keys, preferred_element_type=jnp.float32) * DH ** (
        -0.5
    )
    valid = first + jnp.arange(span, dtype=jnp.int32) < length
    top = jnp.max(jnp.where(valid, scores, NEG), axis=-1)
    weights = jnp.where(valid, jnp.exp(scores - top[..., None]), 0.0)
    total = jnp.sum(weights, axis=-1)
    out = jnp.einsum(
        "rkgt,tkd->rkgd", weights.astype(jnp.bfloat16), values, preferred_element_type=jnp.float32
    )
    return (out.reshape(rows, HQ * DH), top.reshape(rows, HQ), total.reshape(rows, HQ))


def normalize(base, attended, gain):
    mid = (base.astype(jnp.float32) + attended.astype(jnp.float32)).astype(jnp.bfloat16)
    midf = lax.optimization_barrier(mid).astype(jnp.float32)
    factor = lax.rsqrt(jnp.mean(midf * midf, axis=-1, keepdims=True) + EPS)
    return (midf * factor * gain.astype(jnp.float32)).astype(jnp.bfloat16)


def body(
    queries,
    kv_cache,
    tree_kv,
    context_lengths,
    tree_parents,
    resid,
    out_weight,
    norm_gain,
    expert_ids,
    gate_weights,
    w_gate,
    w_up,
    w_down,
):
    here = lax.axis_index("seq")
    parts = lax.axis_size("seq")
    own_rows = queries.shape[1]
    query_all, tree_all, resid_all = (
        lax.all_gather(queries, "seq", axis=1, tiled=True),
        lax.all_gather(tree_kv, "seq", axis=1, tiled=True),
        lax.all_gather(resid, "seq", axis=1, tiled=True),
    )
    query = query_all[0]
    rows = query.shape[0]
    length = context_lengths[0]
    block = kv_cache[0]
    span = block.shape[0]
    out, top, total = shard_partial(query, block, length, here * span)
    got_out, got_top, got_total = (
        lax.all_to_all(out, "seq", split_axis=1, concat_axis=0, tiled=True),
        lax.all_to_all(top, "seq", split_axis=1, concat_axis=0, tiled=True),
        lax.all_to_all(total, "seq", split_axis=1, concat_axis=0, tiled=True),
    )
    mine = HQ // parts
    group = HQ // KVH
    got_out = got_out.reshape(parts, rows, mine, DH)
    got_top = got_top.reshape(parts, rows, mine)
    got_total = got_total.reshape(parts, rows, mine)
    head_ids = here * mine + jnp.arange(mine, dtype=jnp.int32)
    head_pick = ((head_ids // group)[:, None] == jnp.arange(KVH, dtype=jnp.int32)[None, :]).astype(
        jnp.bfloat16
    )
    tree = tree_all[0]
    tree_keys = tree[:, 0].reshape(rows, KVH, DH)
    tree_vals = tree[:, 1].reshape(rows, KVH, DH)
    my_keys = jnp.einsum(
        "nkd,ak->nad", tree_keys, head_pick, preferred_element_type=jnp.float32
    ).astype(jnp.bfloat16)
    my_vals = jnp.einsum(
        "nkd,ak->nad", tree_vals, head_pick, preferred_element_type=jnp.float32
    ).astype(jnp.bfloat16)
    my_query = lax.dynamic_slice_in_dim(query, here * mine * DH, mine * DH, 1).reshape(
        rows, mine, DH
    )
    tree_scores = jnp.einsum(
        "rad,nad->ran", my_query, my_keys, preferred_element_type=jnp.float32
    ) * DH ** (-0.5)
    linked = ancestry(tree_parents[0])[:, None, :]
    tree_top = jnp.max(jnp.where(linked, tree_scores, NEG), axis=-1)
    tree_weights = jnp.where(linked, jnp.exp(tree_scores - tree_top[..., None]), 0.0)
    tree_total = jnp.sum(tree_weights, axis=-1)
    tree_out = jnp.einsum(
        "ran,nad->rad",
        tree_weights.astype(jnp.bfloat16),
        my_vals,
        preferred_element_type=jnp.float32,
    )
    peak = jnp.maximum(jnp.max(got_top, axis=0), tree_top)
    factor = jnp.exp(got_top - peak[None])
    tree_factor = jnp.exp(tree_top - peak)
    numer = jnp.sum(factor[..., None] * got_out, axis=0) + tree_factor[..., None] * tree_out
    denom = jnp.sum(factor * got_total, axis=0) + tree_factor * tree_total
    attention = (numer / denom[..., None]).astype(jnp.bfloat16).reshape(rows, mine * DH)
    projected = jnp.dot(attention, out_weight, preferred_element_type=jnp.float32)
    summed = lax.psum(projected, "seq")
    attended_all = summed.astype(jnp.bfloat16)
    normed = normalize(resid_all[0], attended_all, norm_gain)
    attended = lax.dynamic_slice_in_dim(attended_all, here * own_rows, own_rows, 0)
    ids = expert_ids[0]
    gates = gate_weights[0]
    table = jnp.arange(EXPERTS, dtype=jnp.int32)
    hits = ids[:, :, None] == table[None, None, :]
    choose = jnp.sum(hits.astype(jnp.int32), axis=1)
    weight = jnp.sum(jnp.where(hits, gates[:, :, None], jnp.zeros((), jnp.bfloat16)), axis=1)
    slot = jnp.cumsum(choose, axis=0) - choose
    groups = lax.axis_size("req")
    held = w_gate.shape[0]
    target = jnp.arange(groups, dtype=jnp.int32)[:, None]
    local = jnp.arange(held, dtype=jnp.int32)[None, :]
    owner = ((target * parts + here) * held + local) // SPLIT
    owned = (owner[:, :, None] == table[None, None, :])[..., None]
    chosen = jnp.sum(jnp.where(owned, choose.T[None, None], 0), axis=2)
    seated = jnp.sum(jnp.where(owned, slot.T[None, None], 0), axis=2)
    rate = jnp.sum(jnp.where(owned, weight.T[None, None], jnp.zeros((), jnp.bfloat16)), axis=2)
    seats = jnp.arange(CAP, dtype=jnp.int32)
    select = (chosen[:, :, None, :] > 0) & (seated[:, :, None, :] == seats[None, None, :, None])
    select_b = select.astype(jnp.bfloat16)
    send_rows = jnp.einsum(
        "ghci,id->ghcd", select_b, normed, preferred_element_type=jnp.float32
    ).astype(jnp.bfloat16)
    send_rate = jnp.einsum(
        "ghci,ghi->ghc", select_b, rate, preferred_element_type=jnp.float32
    ).astype(jnp.bfloat16)
    got_rows = lax.all_to_all(send_rows, "req", split_axis=0, concat_axis=0, tiled=True)
    got_rate = lax.all_to_all(send_rate, "req", split_axis=0, concat_axis=0, tiled=True)
    gate = jnp.einsum("shcd,hdf->shcf", got_rows, w_gate, preferred_element_type=jnp.float32)
    up = jnp.einsum("shcd,hdf->shcf", got_rows, w_up, preferred_element_type=jnp.float32)
    hidden = (jax.nn.silu(gate) * up * got_rate[..., None].astype(jnp.float32)).astype(jnp.bfloat16)
    part = jnp.einsum("shcf,hfd->shcd", hidden, w_down, preferred_element_type=jnp.float32).astype(
        jnp.bfloat16
    )
    back = lax.all_to_all(part, "req", split_axis=0, concat_axis=0, tiled=True)
    mixed = jnp.einsum("ghci,ghcd->id", select_b, back, preferred_element_type=jnp.float32)
    expert_rows = lax.psum_scatter(
        mixed.astype(jnp.bfloat16), "seq", scatter_dimension=0, tiled=True
    )
    return (attended[None], expert_rows[None])


def solution(mesh):
    placed = (
        P("req", "seq", None),
        P("req", "seq", None, None),
        P("req", "seq", None, None),
        P("req"),
        P("req", None),
        P("req", "seq", None),
        P("seq", None),
        P(),
        P("req", None, None),
        P("req", None, None),
        P(("req", "seq"), None, None),
        P(("req", "seq"), None, None),
        P(("req", "seq"), None, None),
    )
    return jax.shard_map(
        body,
        mesh=mesh,
        in_specs=placed,
        out_specs=(P("req", "seq", None), P("req", "seq", None)),
        check_vma=False,
    )
```

profile of v0, /device:TPU:1, one launch (start us, length us, event | category | flops | bytes accessed | tf_op | source)
XLA Modules:
  0.0 757.8 jit_solution(11993497939107763333)
XLA Ops:
  7.2 1.5 copy.74
  10.3 34.1 %all_gather.10 = bf16[1,128,2,256]{3,2,0,1:T(2,128)(2,1)S(1)} all-gather(bf16[1,4,2,256]{3,2,0,1:T(2,128)(2,1)} %bitcast.247), channel_id=1, replica_groups=mesh['req'=16,'seq'=32] {'seq'}, dimensions={1}, use_global_device_ids=true | all-gather | bytes 135168 | tf_op jit(solution)/shard_map/all_gather | solution.py:78
  46.5 48.6 %all-gather.3.cloned.1.call-done = bf16[1,128,4096]{2,0,1:T(2,128)(2,1)} async-done(((bf16[1,4,4096]{2,0,1:T(2,128)(2,1)}), bf16[1,128,4096]{2,0,1:T(2,128)(2,1)}) %all-gather.3.cloned.1.call-update) | async-done | bytes 1048592 | tf_op jit(solution)/shard_map/all_gather | solution.py:77
  95.1 5.0 copy.75
  100.1 5.3 fusion
  105.4 5.5 all-to-all-start
  110.9 5.1 fusion.3
  116.0 3.4 all-to-all-done
  119.5 5.8 all-to-all-start.2
  125.3 7.3 fusion.13
  133.8 8.1 %all-to-all-start.1 = ((f32[128,32,128]{2,0,1:T(8,128)}), f32[128,32,128]{2,0,1:T(8,128)S(1)}, u32[]{:S(2)}, u32[]{:S(2)}) async-start(f32[128,32,128]{2,0,1:T(8,128)} %bitcast.231), calls=%async_computation.1 | async-start | bytes 4194304 | tf_op jit(solution)/shard_map/all_to_all | solution.py:88
  148.5 47.1 %all-to-all-done.1 = f32[128,32,128]{2,0,1:T(8,128)S(1)} async-done(((f32[128,32,128]{2,0,1:T(8,128)}), f32[128,32,128]{2,0,1:T(8,128)S(1)}, u32[]{:S(2)}, u32[]{:S(2)}) %all-to-all-start.1) | async-done | bytes 2097184 | tf_op jit(solution)/shard_map/all_to_all | solution.py:88
  195.7 14.6 %all-to-all-start.4 = ((bf16[16,1,32]{2,1,0:T(2,128)(2,1)}), bf16[16,1,32]{2,1,0:T(2,128)(2,1)S(1)}, u32[]{:S(2)}, u32[]{:S(2)}) async-start(bf16[16,1,32]{2,1,0:T(2,128)(2,1)} %copy.93), calls=%async_computation.4 | async-start | bytes 16384 | tf_op jit(solution)/shard_map/all_to_all | solution.py:163
  211.1 1.9 fusion.66
  213.0 140.1 %all-reduce.5 = bf16[128,4096]{1,0:T(8,128)(2,1)} all-reduce(f32[128,4096]{1,0:T(8,128)S(1)} %fusion.66), channel_id=1, replica_groups=mesh['req'=16,'seq'=32] {'seq'}, use_global_device_ids=true, to_apply=%region_7.8 | all-reduce | flops 524288 | bytes 3145728 | tf_op jit(solution)/shard_map/psum | solution.py:133
  353.2 3.1 fusion.19
  356.6 3.3 fusion.5
  359.9 31.8 %all-to-all-start.3 = ((bf16[16,1,32,4096]{3,2,1,0:T(8,128)(2,1)}), bf16[16,1,32,4096]{3,2,1,0:T(8,128)(2,1)}, u32[]{:S(2)}, u32[]{:S(2)}) async-start(bf16[16,1,32,4096]{3,2,1,0:T(8,128)(2,1)} %fusion.5), calls=%async_computation.3 | async-start | bytes 8388608 | tf_op jit(solution)/shard_map/all_to_all | solution.py:162
  391.9 93.4 %all-to-all-done.3 = bf16[16,1,32,4096]{3,2,1,0:T(8,128)(2,1)} async-done(((bf16[16,1,32,4096]{3,2,1,0:T(8,128)(2,1)}), bf16[16,1,32,4096]{3,2,1,0:T(8,128)(2,1)}, u32[]{:S(2)}, u32[]{:S(2)}) %all-to-all-start.3) | async-done | bytes 4194336 | tf_op jit(solution)/shard_map/all_to_all | solution.py:162
  485.3 3.4 fusion.21
  488.8 8.6 %fusion.6 = bf16[16,1,32,4096]{3,2,1,0:T(8,128)(2,1)} fusion(bf16[1,128,4096]{2,1,0:T(8,128)(2,1)S(1)} %copy-done, bf16[16,1,32,4096]{3,2,1,0:T(8,128)(2,1)} %all-to-all-done.3, bf16[1,4096,128]{2,1,0:T(8,128)(2,1)S(1)} %copy-done.1, f32[16,1,32,128]{3,2,0,1:T(8,128)S(1)} %fusion.21, f32[16,32]{1,0:T(8,128)S(1)} %bitcast.243), kind=kOutput, calls=%fused_computation.10 | convolution fusion | flops 1076297728 | bytes 10749952 | tf_op jit(solution)/shard_map/shcf,hfd->shcd/dot_general | solution.py:167
  497.4 101.4 %all_to_all.60 = bf16[16,1,32,4096]{3,2,1,0:T(8,128)(2,1)S(1)} all-to-all(bf16[16,1,32,4096]{3,2,1,0:T(8,128)(2,1)} %fusion.6), channel_id=1, replica_groups=mesh['req'=16,'seq'=32] {'req'}, dimensions={0} | all-to-all | bytes 8388608 | tf_op jit(solution)/shard_map/all_to_all | solution.py:170
  598.7 1.8 fusion.7
  604.0 145.8 %all-reduce.4.cloned.1.call-done = bf16[128,4096]{1,0:T(8,128)(2,1)} async-done(((bf16[128,4096]{1,0:T(8,128)(2,1)}), bf16[128,4096]{1,0:T(8,128)(2,1)}) %all-reduce.4.cloned.1.call-update) | async-done | bytes 1048592
  (67 shorter events, 16.1 us)
Async XLA Ops:
  7.2 481.6 %copy-start = (bf16[1,128,4096]{2,1,0:T(8,128)(2,1)S(1)}, bf16[1,128,4096]{2,1,0:T(8,128)(2,1)}, u32[]{:S(2)}) copy-start(bf16[1,128,4096]{2,1,0:T(8,128)(2,1)} %param.25) | copy-start | bytes 3145732
  7.2 87.9 %all-gather.3.cloned.1.call-start = ((), (), s32[]{:S(2)}) async-start(), calls=%async_computation.6 | async-start | bytes 2162688 | tf_op jit(solution)/shard_map/all_gather | solution.py:77
  8.8 344.4 %all-gather.5.cloned.1.call-start = ((), (), s32[]{:S(2)}) async-start(), calls=%async_computation.7 | async-start | bytes 2162688 | tf_op jit(solution)/shard_map/all_gather | solution.py:79
  105.4 14.1 %all-to-all-start = ((f32[128,32,1]{0,2,1:T(1,128)}), f32[128,32,1]{0,2,1:T(1,128)S(1)}, u32[]{:S(2)}, u32[]{:S(2)}) async-start(f32[128,32,1]{0,2,1:T(1,128)} %bitcast.12), calls=%async_computation | async-start | bytes 32768 | tf_op jit(solution)/shard_map/all_to_all | solution.py:89
  119.5 14.3 %all-to-all-start.2 = ((f32[128,32,1]{0,2,1:T(1,128)}), f32[128,32,1]{0,2,1:T(1,128)S(1)}, u32[]{:S(2)}, u32[]{:S(2)}) async-start(f32[128,32,1]{0,2,1:T(1,128)} %bitcast.39), calls=%async_computation.2 | async-start | bytes 32768 | tf_op jit(solution)/shard_map/all_to_all | solution.py:90
  132.6 10.3 %copy-start.3 = (s32[1,128,8]{1,2,0:T(8,128)S(1)}, s32[1,128,8]{1,2,0:T(8,128)}, u32[]{:S(2)}) copy-start(s32[1,128,8]{1,2,0:T(8,128)} %param.21) | copy-start | bytes 12292
  132.6 10.7 %copy-start.4 = (bf16[4096]{0:T(1024)(128)(2,1)S(1)}, bf16[4096]{0:T(1024)(128)(2,1)}, u32[]{:S(2)}) copy-start(bf16[4096]{0:T(1024)(128)(2,1)} %param.20) | copy-start | bytes 24580
  132.6 10.7 %copy-start.5 = (bf16[1,128,8]{1,2,0:T(8,128)(2,1)S(1)}, bf16[1,128,8]{1,2,0:T(8,128)(2,1)}, u32[]{:S(2)}) copy-start(bf16[1,128,8]{1,2,0:T(8,128)(2,1)} %param.22) | copy-start | bytes 6148
  132.6 12.1 %copy-start.6 = (s32[1,128]{1,0:T(1,128)S(1)}, s32[1,128]{1,0:T(1,128)}, u32[]{:S(2)}) copy-start(s32[1,128]{1,0:T(1,128)} %param.17) | copy-start | bytes 1540
  133.8 61.9 %all-to-all-start.1 = ((f32[128,32,128]{2,0,1:T(8,128)}), f32[128,32,128]{2,0,1:T(8,128)S(1)}, u32[]{:S(2)}, u32[]{:S(2)}) async-start(f32[128,32,128]{2,0,1:T(8,128)} %bitcast.231), calls=%async_computation.1 | async-start | bytes 4194304 | tf_op jit(solution)/shard_map/all_to_all | solution.py:88
  195.7 164.3 %all-to-all-start.4 = ((bf16[16,1,32]{2,1,0:T(2,128)(2,1)}), bf16[16,1,32]{2,1,0:T(2,128)(2,1)S(1)}, u32[]{:S(2)}, u32[]{:S(2)}) async-start(bf16[16,1,32]{2,1,0:T(2,128)(2,1)} %copy.93), calls=%async_computation.4 | async-start | bytes 16384 | tf_op jit(solution)/shard_map/all_to_all | solution.py:163
  359.9 125.4 %copy-start.2 = (bf16[1,4096,128]{2,1,0:T(8,128)(2,1)S(1)}, bf16[1,4096,128]{2,1,0:T(8,128)(2,1)}, u32[]{:S(2)}) copy-start(bf16[1,4096,128]{2,1,0:T(8,128)(2,1)} %param.23) | copy-start | bytes 3145732
  359.9 125.4 %all-to-all-start.3 = ((bf16[16,1,32,4096]{3,2,1,0:T(8,128)(2,1)}), bf16[16,1,32,4096]{3,2,1,0:T(8,128)(2,1)}, u32[]{:S(2)}, u32[]{:S(2)}) async-start(bf16[16,1,32,4096]{3,2,1,0:T(8,128)(2,1)} %fusion.5), calls=%async_computation.3 | async-start | bytes 8388608 | tf_op jit(solution)/shard_map/all_to_all | solution.py:162
  391.8 97.0 %copy-start.1 = (bf16[1,4096,128]{2,1,0:T(8,128)(2,1)S(1)}, bf16[1,4096,128]{2,1,0:T(8,128)(2,1)}, u32[]{:S(2)}) copy-start(bf16[1,4096,128]{2,1,0:T(8,128)(2,1)} %param.24) | copy-start | bytes 3145732
  391.8 358.0 %all-reduce.4.cloned.1.call-start = ((), (), s32[]{:S(2)}) async-start(), calls=%async_computation.8 | async-start | bytes 2097152
Sparse Core Ops, SparseCore 0:
  11.2 83.8 all-gather.2
  98.3 94.6 all-gather.4
  600.7 149.0 all-reduce.3
where the time goes:
time: 762 us; the launch traced here: 758 us
  waiting for transfers between devices  340 us (45%)
  blocking collectives  276 us (36%)
  starting transfers between devices  66 us (9%)
  matrix products  34.5 us (5%)
  local copies, waits for them, and re-layouts  16.4 us (2%)
  between operations  15.3 us (2%)
  other arithmetic  10.4 us (1%)
    unnamed x4, waiting for transfers between devices  146 us
    psum x1, blocking collectives, body(): summed = lax.psum(projected, 'seq')  140 us
    all_to_all x1, blocking collectives, body(): back = lax.all_to_all(part, 'req', split_axis=0, concat_axis=0, tiled=True)  101 us
    all_to_all x1, waiting for transfers between devices, body(): lax.all_to_all(send_rows, 'req', split_axis=0, concat_axis=0, tiled=True)  93.4 us
    all_gather x1, waiting for transfers between devices, body(): lax.all_gather(queries, 'seq', axis=1, tiled=True)  48.6 us
    all_to_all x1, waiting for transfers between devices, body(): lax.all_to_all(out, 'seq', split_axis=1, concat_axis=0, tiled=True)  47.1 us
    all_gather x1, blocking collectives, body(): lax.all_gather(tree_kv, 'seq', axis=1, tiled=True)  34.1 us
    all_to_all x1, starting transfers between devices, body(): lax.all_to_all(send_rows, 'req', split_axis=0, concat_axis=0, tiled=True)  31.8 us
  transfers between devices with their start and end apart: 8, of which 6 were waited for; matrix products, arithmetic and copies ran while one was open for 6% of the time, Pallas kernels for 0%

commit v1 on v0

v1 whole, which is shorter than its diff:
```python
import jax
import jax.numpy as jnp
from jax import lax
from jax.experimental import pallas as pl
from jax.experimental.pallas import tpu as pltpu
from jax.sharding import PartitionSpec as P

BF = jnp.bfloat16
F32 = jnp.float32
MESH = pl.DeviceIdType.MESH
NX, NY = 4, 8
NR, NS = 16, 32
SPAN = 528
KEYS = 2 * SPAN
MASKED = -1e30
FLOOR = -1e29
EPS = 1e-06


def rem(a, b):
    return lax.rem(a, jnp.int32(b))


def div(a, b):
    return lax.div(a, jnp.int32(b))


def place():
    r = lax.axis_index("req")
    s = lax.axis_index("seq")
    return r, s, rem(s, NX), div(s, NX)


def remote(src, dst, send, recv, r, s):
    return pltpu.make_async_remote_copy(
        src_ref=src, dst_ref=dst, send_sem=send, recv_sem=recv, device_id=(r, s), device_id_type=MESH
    )


def loop(n, first=0):
    def run(fn):
        def step(i, c):
            fn(i)
            return c

        lax.fori_loop(first, n, step, 0)

    return run


def dot(a, b):
    return jnp.dot(a, b, preferred_element_type=F32)


def gather_kernel(q_in, kv_in, res_in, link, q_out, kv_out, res_out, reach_out,
                  qy, reach, ys, yr, xs, xr, ks, rs, rr, ls):
    r, s, x, y = place()
    h = rem(x, 2)
    mate = s + 1 - 2 * h
    barrier = pltpu.get_barrier_semaphore()

    @loop(NS, 1)
    def _(d):
        pl.semaphore_signal(barrier, inc=1, device_id=(r, rem(s + d, NS)), device_id_type=MESH)

    pl.semaphore_wait(barrier, NS - 1)

    def y_copy(d):
        return remote(q_in, qy.at[y], ys.at[d], yr.at[d], r, rem(y + d, NY) * NX + x)

    def kv_copy():
        return remote(kv_in.at[1 - h], kv_out.at[h], ks.at[0], ks.at[1], r, mate)

    def res_copy(d):
        to = rem(s + d, NS)
        return remote(res_in.at[to], res_out.at[s], rs.at[d], rr.at[d], r, to)

    def x_copy(d, e):
        row = rem(y + NY - d, NY)
        to = rem(x + e, NX)
        return remote(qy.at[row, rem(to, 2)], q_out.at[row * NX + x], xs.at[d, e], xr.at[d, e], r, y * NX + to)

    @loop(NY, 1)
    def _(d):
        y_copy(d).start()

    kv_copy().start()
    own_q = pltpu.make_async_copy(q_in, qy.at[y], ls.at[0])
    own_q.start()
    own_kv = pltpu.make_async_copy(kv_in.at[h], kv_out.at[h], ls.at[1])
    own_kv.start()
    own_res = pltpu.make_async_copy(res_in.at[s], res_out.at[s], ls.at[2])
    own_res.start()
    own_q.wait()

    def spread(d):
        for e in range(1, NX):
            x_copy(d, e).start()
        row = rem(y + NY - d, NY)
        pltpu.make_async_copy(qy.at[row, h], q_out.at[row * NX + x], xs.at[d, 0]).start()

    spread(0)

    @loop(NS, 1)
    def _(d):
        res_copy(d).start()

    @loop(NY, 1)
    def _(d):
        y_copy(d).wait_recv()
        spread(d)

    reach[...] = link[...]

    @loop(5)
    def _(i):
        reach[...] = jnp.minimum(dot(reach[...], reach[...]), 1.0).astype(BF)

    reach_out[...] = reach[...]
    own_kv.wait()
    own_res.wait()
    kv_copy().wait()

    @loop(NY, 1)
    def _(d):
        y_copy(d).wait_send()

    @loop(NS, 1)
    def _(d):
        res_copy(d).wait()

    @loop(NY)
    def _(d):
        for e in range(1, NX):
            x_copy(d, e).wait()
        row = rem(y + NY - d, NY)
        pltpu.make_async_copy(qy.at[row, h], q_out.at[row * NX + x], xs.at[d, 0]).wait()


def main_kernel(
    q, k, vt, bias, res, w_out, gain, sel, back, w_gate, w_up, w_down,
    a_out, e_out,
    out_src, st_src, got, got_st, p_src, p_got, y_src, y_got, a_src, sq_src, sq, mid_src, mid_q,
    d_src, rows, wgu, wd, gu_src, gu, hid_src, hid, pair_src, pair, ret_src, ret, f_src, fin,
    hs, hr, ts, tr, ps, pr, ys, yr, as_, ar, qs, qr, ms, mr, zs, zr, fs, fr,
    gs, gr, us, ur, ds_, dr, gus, gur, hds, hdr, pas, par, bs, br, es, er, ls,
):
    r, s, x, y = place()
    h = rem(x, 2)
    b = rem(y, 2)
    top = div(y, 4)
    mate = s + NX - 2 * NX * b
    number = y * 2 + div(x, 2)
    barrier = pltpu.get_barrier_semaphore()

    @loop(NS, 1)
    def _(d):
        pl.semaphore_signal(barrier, inc=1, device_id=(r, rem(s + d, NS)), device_id_type=MESH)

    @loop(NR, 1)
    def _(d):
        pl.semaphore_signal(barrier, inc=1, device_id=(rem(r + d, NR), s), device_id_type=MESH)

    pl.semaphore_wait(barrier, NS + NR - 2)

    def x_at(e):
        return rem(x + e, NX)

    def gate_copy(e):
        to = x_at(e)
        return remote(w_gate.at[to], wgu.at[x, :, pl.ds(0, 128)], gs.at[e], gr.at[e], r, y * NX + to)

    def up_copy(e):
        to = x_at(e)
        return remote(w_up.at[to], wgu.at[x, :, pl.ds(128, 128)], us.at[e], ur.at[e], r, y * NX + to)

    def down_copy(e):
        to = x_at(e)
        return remote(
            w_down.at[:, pl.ds(pl.multiple_of(to * 1024, 1024), 1024)], wd.at[x], ds_.at[e], dr.at[e], r, y * NX + to
        )

    own_g = pltpu.make_async_copy(w_gate.at[x], wgu.at[x, :, pl.ds(0, 128)], ls.at[0])
    own_u = pltpu.make_async_copy(w_up.at[x], wgu.at[x, :, pl.ds(128, 128)], ls.at[1])
    own_d = pltpu.make_async_copy(w_down.at[:, pl.ds(pl.multiple_of(x * 1024, 1024), 1024)], wd.at[x], ls.at[2])
    own_g.start()
    own_u.start()
    own_d.start()

    def out_copy(i):
        return remote(out_src.at[i], got.at[number], hs.at[i], hr.at[number], r, 16 * h + i)

    def st_copy(i):
        return remote(st_src.at[i], got_st.at[number], ts.at[i], tr.at[number], r, 16 * h + i)

    def local_out(i):
        return (
            pltpu.make_async_copy(out_src.at[i], got.at[number], hs.at[i]),
            pltpu.make_async_copy(st_src.at[i], got_st.at[number], ts.at[i]),
        )

    def head_at(n):
        return rem(n + number, 16)

    def send_head(i):
        @pl.when(16 * h + i != s)
        def _():
            out_copy(i).start()
            st_copy(i).start()

        @pl.when(16 * h + i == s)
        def _():
            one, two = local_out(i)
            one.start()
            two.start()

    @loop(16)
    def _(n):
        i = head_at(n)
        heads = q[:, pl.ds(pl.multiple_of(i * 128, 128), 128)]
        score = lax.dot_general(k[...], heads, (((1,), (1,)), ((), ())), preferred_element_type=F32)
        score = score * (128 ** (-0.5)) + bias[...]
        peak = jnp.maximum(jnp.max(score, axis=0, keepdims=True), FLOOR)
        prob = jnp.exp(score - peak)
        total = jnp.sum(prob, axis=0, keepdims=True)
        out_src[i] = dot(vt[...], prob.astype(BF)).astype(BF)
        st_src[i] = jnp.concatenate([jnp.broadcast_to(peak, (8, 128)), jnp.broadcast_to(total, (8, 128))], axis=0)

        @pl.when(n >= 1)
        def _():
            send_head(head_at(n + 15))

    send_head(head_at(jnp.int32(15)))

    for e in range(1, NX):
        gate_copy(jnp.int32(e)).start()

    def wait_source(n):
        who = div(n, 2) * NX + 2 * rem(n, 2) + top

        @pl.when(who != s)
        def _():
            remote(out_src.at[0], got.at[n], hs.at[0], hr.at[n], r, who).wait_recv()
            remote(st_src.at[0], got_st.at[n], ts.at[0], tr.at[n], r, who).wait_recv()

    @loop(16)
    def _(n):
        wait_source(n)

    @loop(16)
    def _(n):
        i = head_at(n)

        @pl.when(16 * h + i != s)
        def _():
            out_copy(i).wait_send()
            st_copy(i).wait_send()

        @pl.when(16 * h + i == s)
        def _():
            one, two = local_out(i)
            one.wait()
            two.wait()

    peaks = got_st[:, 0:1, :]
    totals = got_st[:, 8:9, :]
    peak = jnp.max(peaks, axis=0)
    factor = jnp.exp(peaks - peak[None])
    denom = jnp.sum(factor * totals, axis=0)
    numer = jnp.zeros((128, 128), F32)
    for n in range(16):
        numer = numer + factor[n] * got[n].astype(F32)
    att = jnp.transpose(numer / denom).astype(BF)

    def p_copy(e):
        return remote(p_src.at[e], p_got.at[e], ps.at[e], pr.at[e], r, y * NX + x_at(e))

    for e in (1, 2, 3, 0):
        cols = pl.multiple_of(x_at(jnp.int32(e)) * 1024, 1024)
        part = dot(att, w_out[:, pl.ds(cols, 1024)]).astype(BF)
        p_src[e] = part
        if e:
            p_copy(e).start()
    for e in range(1, NX):
        up_copy(jnp.int32(e)).start()
    for e in range(1, NX):
        down_copy(jnp.int32(e)).start()
    for e in range(1, NX):
        p_copy(e).wait_recv()

    def y_copy(d):
        to = rem(y + d, NY)
        return remote(y_src.at[to], y_got.at[d], ys.at[d], yr.at[d], r, to * NX + x)

    for t in range(NY):
        c = slice(128 * t, 128 * t + 128)
        acc = p_src[0, :, c].astype(F32)
        for e in range(1, NX):
            acc = acc + p_got[e, :, c].astype(F32)
        y_src[t] = acc.astype(BF)

    @loop(NY, 1)
    def _(d):
        y_copy(d).start()

    acc = y_src[y].astype(F32)
    for d in range(1, NY):
        y_copy(jnp.int32(d)).wait_recv()
        acc = acc + y_got[d].astype(F32)
    attended = acc.astype(BF)
    mid = (res[...].astype(F32) + attended.astype(F32)).astype(BF)
    midf = mid.astype(F32)
    mid_src[...] = mid
    col = jnp.sum(midf * midf, axis=1, keepdims=True)
    sq_src[...] = jnp.transpose(jnp.broadcast_to(col, (128, 128)))[0:8, :]
    sq[s] = sq_src[...]
    wide = attended.astype(F32)
    for t in range(NS):
        a_src[t] = wide[4 * t : 4 * t + 4, :].astype(BF)

    def mid_copy(j):
        to = (2 * j + top) * NX + x
        return remote(mid_src, mid_q.at[rem(y, 4)], ms.at[j], mr.at[rem(y, 4)], r, to)

    def sq_copy(d):
        return remote(sq_src, sq.at[s], qs.at[d], qr.at[d], r, rem(s + d, NS))

    def a_copy(d):
        to = rem(s + d, NS)
        return remote(a_src.at[to], a_out.at[s], as_.at[d], ar.at[d], r, to)

    mine = pltpu.make_async_copy(mid_src, mid_q.at[rem(y, 4)], ls.at[3])

    @loop(NS, 1)
    def _(d):
        sq_copy(d).start()

    @loop(4)
    def _(j):
        @pl.when(2 * j + top != y)
        def _():
            mid_copy(j).start()

        @pl.when(2 * j + top == y)
        def _():
            mine.start()

    a_out[s] = a_src[s]

    @loop(NS, 1)
    def _(d):
        a_copy(d).start()

    @loop(4)
    def _(t):
        @pl.when(4 * b + t != y)
        def _():
            remote(mid_src, mid_q.at[t], ms.at[0], mr.at[t], r, (4 * b + t) * NX + x).wait_recv()

        @pl.when(4 * b + t == y)
        def _():
            mine.wait()

    @loop(NS, 1)
    def _(d):
        sq_copy(d).wait_recv()

    square = jnp.sum(sq[:, 0:1, :], axis=0)
    scale = lax.rsqrt(square * (1.0 / 4096.0) + EPS)
    scale = jnp.transpose(jnp.broadcast_to(scale, (128, 128)))
    for t in range(4):
        normed = (mid_q[t].astype(F32) * scale * gain[t]).astype(BF)
        d_src[:, :, 128 * t : 128 * t + 128] = dot(sel[...], normed).astype(BF).reshape(16, 32, 128)

    def z_copy(d):
        to = rem(r + d, NR)
        return remote(d_src.at[to], rows.at[b, r], zs.at[d], zr.at[d], to, s)

    def pass_copy(d):
        who = rem(r + NR - d, NR)
        return remote(rows.at[b, who], rows.at[b, who], fs.at[d], fr.at[d], r, mate)

    own_rows = pltpu.make_async_copy(d_src.at[r], rows.at[b, r], ls.at[4])
    own_rows.start()

    @loop(NR, 1)
    def _(d):
        z_copy(d).start()

    own_rows.wait()
    pass_copy(jnp.int32(0)).start()

    @loop(NR, 1)
    def _(d):
        z_copy(d).wait_recv()
        pass_copy(d).start()

    own_g.wait()
    own_u.wait()
    own_d.wait()
    for e in range(1, NX):
        gate_copy(jnp.int32(e)).wait()
        up_copy(jnp.int32(e)).wait()

    @loop(NR)
    def _(d):
        who = rem(r + NR - d, NR)
        remote(rows.at[1 - b, who], rows.at[1 - b, who], fs.at[d], fr.at[d], r, mate).wait_recv()

    def gu_copy(e):
        return remote(gu_src.at[e], gu.at[e], gus.at[e], gur.at[e], r, y * NX + x_at(e))

    for e in (1, 2, 3, 0):
        to = x_at(jnp.int32(e))

        @loop(4)
        def _(m):
            left = rows[0, pl.ds(4 * m, 4)].reshape(128, 512)
            right = rows[1, pl.ds(4 * m, 4)].reshape(128, 512)
            part = dot(left, wgu[to, 0:512, :]) + dot(right, wgu[to, 512:1024, :])
            gu_src[e, pl.ds(pl.multiple_of(128 * m, 128), 128), :] = part.astype(BF)

        if e:
            gu_copy(e).start()
    for e in range(1, NX):
        gu_copy(e).wait_recv()

    @loop(4)
    def _(m):
        part = pl.ds(pl.multiple_of(128 * m, 128), 128)
        acc = gu_src[0, part, :].astype(F32)
        for e in range(1, NX):
            acc = acc + gu[e, part, :].astype(F32)
        gate = acc[:, 0:128]
        hid_src[part, :] = (gate / (1.0 + jnp.exp(-gate)) * acc[:, 128:256]).astype(BF)

    def hid_copy(e):
        return remote(hid_src, hid.at[x], hds.at[e], hdr.at[e], r, y * NX + x_at(e))

    own_hid = pltpu.make_async_copy(hid_src, hid.at[x], ls.at[5])
    own_hid.start()
    for e in range(1, NX):
        hid_copy(e).start()
    for e in range(1, NX):
        down_copy(jnp.int32(e)).wait()
    own_hid.wait()
    for e in range(1, NX):
        hid_copy(e).wait_recv()

    def down(m, half):
        part = pl.ds(pl.multiple_of(128 * m, 128), 128)
        cols = pl.ds(pl.multiple_of(half * 512, 512), 512)
        acc = dot(hid[0, part, :], wd[0, :, cols])
        for t in range(1, NX):
            acc = acc + dot(hid[t, part, :], wd[t, :, cols])
        return acc

    def pair_copy(m):
        part = pl.ds(pl.multiple_of(128 * m, 128), 128)
        return remote(pair_src.at[part], pair.at[part], pas.at[m], par.at[m], r, mate)

    @loop(4)
    def _(m):
        part = pl.ds(pl.multiple_of(128 * m, 128), 128)
        pair_src[part, :] = down(m, 1 - b).astype(BF)
        pair_copy(m).start()

    def b_copy(to):
        return remote(ret_src.at[to], ret.at[r], bs.at[to], br.at[r], to, s)

    @loop(4)
    def _(m):
        part = pl.ds(pl.multiple_of(128 * m, 128), 128)
        acc = down(m, b)
        pair_copy(m).wait_recv()
        acc = acc + pair[part, :].astype(F32)
        ret_src[pl.ds(4 * m, 4)] = acc.astype(BF).reshape(4, 32, 512)
        for t in range(4):
            to = 4 * m + t

            @pl.when(to != r)
            def _():
                b_copy(to).start()

    ret[r] = ret_src[r]

    @loop(NR)
    def _(n):
        @pl.when(n != r)
        def _():
            remote(ret_src.at[0], ret.at[n], bs.at[0], br.at[n], n, s).wait_recv()

    total = dot(back[...], ret[...].reshape(512, 512))
    for t in range(NS):
        f_src[t] = total[4 * t : 4 * t + 4, :].astype(BF)

    def f_copy(d):
        to = rem(s + d, NS)
        return remote(f_src.at[to], fin.at[s], es.at[d], er.at[d], r, to)

    fin[s] = f_src[s]

    @loop(NS, 1)
    def _(d):
        f_copy(d).start()

    for e in range(1, NX):
        p_copy(e).wait_send()
        gu_copy(e).wait_send()
        hid_copy(e).wait_send()

    @loop(NY, 1)
    def _(d):
        y_copy(d).wait_send()

    @loop(4)
    def _(j):
        @pl.when(2 * j + top != y)
        def _():
            mid_copy(j).wait_send()

    @loop(NS, 1)
    def _(d):
        sq_copy(d).wait_send()
        a_copy(d).wait()

    @loop(NR, 1)
    def _(d):
        z_copy(d).wait_send()

    @loop(NR)
    def _(d):
        pass_copy(d).wait_send()

    @loop(4)
    def _(m):
        pair_copy(m).wait_send()

    @loop(NR)
    def _(n):
        @pl.when(n != r)
        def _():
            b_copy(n).wait_send()

    @loop(NS, 1)
    def _(d):
        f_copy(d).wait()

    for xx in range(NX):
        for bb in range(2):
            acc = fin[bb * NX + xx].astype(F32)
            for j in range(1, 4):
                acc = acc + fin[(2 * j + bb) * NX + xx].astype(F32)
            e_out[:, 1024 * xx + 512 * bb : 1024 * xx + 512 * bb + 512] = acc.astype(BF)


VM = pl.BlockSpec(memory_space=pltpu.VMEM)
HB = pl.BlockSpec(memory_space=pl.ANY)


def sds(shape, dtype=BF):
    return jax.ShapeDtypeStruct(shape, dtype)


def dma(*shape):
    return pltpu.SemaphoreType.DMA(shape)


def body(
    queries, kv_cache, tree_kv, context_lengths, tree_parents, resid, out_weight, norm_gain,
    expert_ids, gate_weights, w_gate, w_up, w_down,
):
    r, s, x, y = place()
    j = div(y, 2)
    b = rem(y, 2)
    h = rem(x, 2)
    q_in = queries[0].reshape(4, 2, 2048).transpose(1, 0, 2)
    both = jnp.concatenate([kv_cache[0], tree_kv[0], jnp.zeros((12, 2, 256), BF)], axis=0)
    kv_in = both.reshape(SPAN, 2, 2, 128).transpose(2, 1, 0, 3)
    res_in = resid[0].reshape(4, NX, NY, 128).transpose(2, 1, 0, 3).reshape(NS, 4, 128)
    parents = tree_parents[0]
    node = jnp.arange(128, dtype=jnp.int32)
    link = ((parents[None, :] == node[:, None]) | (node[:, None] == node[None, :])).astype(BF)
    q_out, kv_out, res_out, reach = pl.pallas_call(
        gather_kernel,
        name="gather",
        out_shape=(sds((NS, 4, 2048)), sds((2, 2, SPAN, 128)), sds((NS, 4, 128)), sds((128, 128))),
        in_specs=[VM] * 4,
        out_specs=(VM,) * 4,
        scratch_shapes=[
            pltpu.VMEM((NY, 2, 4, 2048), BF), pltpu.VMEM((128, 128), BF),
            dma(NY), dma(NY), dma(NY, NX), dma(NY, NX), dma(2), dma(NS), dma(NS), dma(3),
        ],
        compiler_params=pltpu.CompilerParams(collective_id=0, has_side_effects=True),
    )(q_in, kv_in, res_in, link)
    query = q_out.reshape(128, 2048)
    keys = kv_out[:, 0].reshape(KEYS, 128)
    vals = kv_out[:, 1].reshape(KEYS, 128).T
    base = s - h
    spot = jnp.arange(SPAN, dtype=jnp.int32)
    shard = base + jnp.arange(2, dtype=jnp.int32)[:, None]
    seen = (spot[None, :] < 512) & (shard * 512 + spot[None, :] < context_lengths[0])
    bias = jnp.where(seen, 0.0, MASKED).astype(F32)
    kin = lax.dynamic_slice_in_dim(reach, 4 * base, 8, 0).astype(F32).reshape(2, 4, 128)
    kin = jnp.where(kin > 0.5, 0.0, MASKED)
    bias = jnp.broadcast_to(bias[:, :, None], (2, SPAN, 128))
    bias = lax.dynamic_update_slice(bias, kin, (0, 512, 0)).reshape(KEYS, 128)
    ids, gates = expert_ids[0], gate_weights[0]
    mine = 4 * jnp.arange(16, dtype=jnp.int32) + j
    hit = ids[None] == mine[:, None, None]
    chosen = jnp.any(hit, axis=2)
    rate = jnp.sum(jnp.where(hit, gates[None].astype(F32), 0.0), axis=2)
    before = (node[:, None] < node[None, :]).astype(BF)
    slot = jnp.dot(chosen.astype(BF), before, preferred_element_type=F32)
    seats = jnp.arange(32, dtype=jnp.int32).astype(F32)
    seated = chosen[:, None, :] & (slot[:, None, :] == seats[None, :, None])
    sel = seated.astype(BF).reshape(512, 128)
    back = jnp.where(seated, rate[:, None, :], 0.0).astype(BF).reshape(512, 128).T
    gain = lax.dynamic_slice_in_dim(norm_gain, x * 1024 + b * 512, 512, 0).astype(F32).reshape(4, 1, 128)
    a_out, e_out = pl.pallas_call(
        main_kernel,
        name="layer",
        out_shape=(sds((NS, 4, 128)), sds((4, 4096))),
        in_specs=[VM] * 9 + [HB] * 3,
        out_specs=(VM, VM),
        scratch_shapes=[
            pltpu.VMEM((16, 128, 128), BF), pltpu.VMEM((16, 16, 128), F32),
            pltpu.VMEM((16, 128, 128), BF), pltpu.VMEM((16, 16, 128), F32),
            pltpu.VMEM((NX, 128, 1024), BF), pltpu.VMEM((NX, 128, 1024), BF),
            pltpu.VMEM((NY, 128, 128), BF), pltpu.VMEM((NY, 128, 128), BF),
            pltpu.VMEM((NS, 4, 128), BF), pltpu.VMEM((8, 128), F32), pltpu.VMEM((NS, 8, 128), F32),
            pltpu.VMEM((128, 128), BF), pltpu.VMEM((4, 128, 128), BF),
            pltpu.VMEM((16, 32, 512), BF), pltpu.VMEM((2, 16, 32, 512), BF),
            pltpu.VMEM((NX, 1024, 256), BF), pltpu.VMEM((NX, 128, 1024), BF),
            pltpu.VMEM((NX, 512, 256), BF), pltpu.VMEM((NX, 512, 256), BF),
            pltpu.VMEM((512, 128), BF), pltpu.VMEM((NX, 512, 128), BF),
            pltpu.VMEM((512, 512), BF), pltpu.VMEM((512, 512), BF),
            pltpu.VMEM((16, 32, 512), BF), pltpu.VMEM((16, 32, 512), BF),
            pltpu.VMEM((NS, 4, 512), BF), pltpu.VMEM((NS, 4, 512), BF),
            dma(16), dma(16), dma(16), dma(16), dma(4), dma(4), dma(8), dma(8),
            dma(NS), dma(NS), dma(NS), dma(NS), dma(4), dma(4), dma(16), dma(16), dma(16), dma(16),
            dma(4), dma(4), dma(4), dma(4), dma(4), dma(4), dma(4), dma(4), dma(4), dma(4),
            dma(4), dma(4), dma(16), dma(16), dma(NS), dma(NS), dma(6),
        ],
        compiler_params=pltpu.CompilerParams(collective_id=1, has_side_effects=True),
    )(
        query, keys, vals, bias, res_out.reshape(128, 128), out_weight, gain, sel, back,
        w_gate[0].reshape(NX, 1024, 128), w_up[0].reshape(NX, 1024, 128), w_down[0],
    )
    attended = a_out.reshape(NY, NX, 4, 128).transpose(2, 1, 0, 3).reshape(1, 4, 4096)
    return attended, e_out[None]


def solution(mesh):
    placed = (
        P("req", "seq", None),
        P("req", "seq", None, None),
        P("req", "seq", None, None),
        P("req"),
        P("req", None),
        P("req", "seq", None),
        P("seq", None),
        P(),
        P("req", None, None),
        P("req", None, None),
        P(("req", "seq"), None, None),
        P(("req", "seq"), None, None),
        P(("req", "seq"), None, None),
    )
    return jax.shard_map(
        body,
        mesh=mesh,
        in_specs=placed,
        out_specs=(P("req", "seq", None), P("req", "seq", None)),
        check_vma=False,
    )
```

time: 762 us -> 200 us (0.26)
  waiting for transfers between devices: 340 us -> 0 us
  blocking collectives: 276 us -> 0 us
  Pallas kernels: 0 us -> 180 us
  starting transfers between devices: 66 us -> 0 us
  matrix products: 34.5 us -> 0.13 us
  between operations: 15.3 us -> 1.46 us
    pallas_call x0 -> x2, Pallas kernels: none -> 180 us  [the longest x1 155 us: body(): pl.pallas_call(main_kernel, name='layer', out_shape=(sds((NS, 4, 128)), s...]
    unnamed x4 -> x0, waiting for transfers between devices: 146 us -> none
    all_to_all x5 -> x0, waiting for transfers between devices: 145 us -> none  [the longest x1 93.4 us: body(): lax.all_to_all(send_rows, 'req', split_axis=0, concat_axis=0, tiled=True)]
    psum x1 -> x0, blocking collectives: 140 us -> none  [body(): summed = lax.psum(projected, 'seq')]
    all_to_all x1 -> x0, blocking collectives: 101 us -> none  [body(): back = lax.all_to_all(part, 'req', split_axis=0, concat_axis=0, tiled=True)]
    all_to_all x5 -> x0, starting transfers between devices: 65.9 us -> none  [the longest x1 31.8 us: body(): lax.all_to_all(send_rows, 'req', split_axis=0, concat_axis=0, tiled=True)]
    all_gather x2 -> x0, waiting for transfers between devices: 48.6 us -> none  [the longest x1 48.6 us: body(): lax.all_gather(queries, 'seq', axis=1, tiled=True)]
    dot_general x15 -> x1, matrix products: 34.5 us -> 0.13 us  [body(): slot = jnp.dot(chosen.astype(BF), before, preferred_element_type=F32)]
  transfers between devices with their start and end apart: 8 -> 0, of which waited for: 6 -> 0; matrix products, arithmetic and copies ran while one was open for 6% -> 0% of each run, Pallas kernels for 0% -> 0%
where the time goes in v1:
time: 200 us; the launch traced here: 198 us
  Pallas kernels  180 us (90%)
  local copies, waits for them, and re-layouts  11 us (6%)
  other arithmetic  4.74 us (2%)
    pallas_call x1, Pallas kernels, body(): pl.pallas_call(main_kernel, name='layer', out_shape=(sds((NS, 4, 128)), s...  155 us
    pallas_call x1, Pallas kernels, body(): pl.pallas_call(gather_kernel, name='gather', out_shape=(sds((NS, 4, 2048)...  25.2 us

profile of v1, /device:TPU:1, one launch (start us, length us, event | category | flops | bytes accessed | tf_op | source)
XLA Modules:
  0.0 197.7 jit_solution(18358152131482513541)
XLA Ops:
  0.6 0.7 concatenate.9
  1.3 1.3 copy.34
  2.7 0.3 copy.35
  3.0 1.0 maximum_bitcast_fusion.kv_in
  4.0 0.6 copy.37
  4.7 0.6 fusion.3.link
  5.3 25.2 %gather.1 = (bf16[32,4,2048]{2,1,0:T(4,128)(2,1)}, bf16[2,2,528,128]{3,2,1,0:T(8,128)(2,1)}, bf16[32,4,128]{2,1,0:T(4,128)(2,1)}, bf16[128,128]{1,0:T(8,128)(2,1)}) custom-call(bf16[2,4,2048]{2,1,0:T(4,128)(2,1)} %bitcast.58, bf16[2,2,528,128]{3,2,1,0:T(8,128)(2,1)} %maximum_bitcast_fusion.kv_in, bf16[32,4,128]{2,1,0:T(4,128)(2,1)} %bitcast.55, ...), custom_call_target="tpu_custom_call" | custom-call | tf_op jit(solution)/shard_map/gather/pallas_call | solution.py:584
  30.5 2.0 %reshape.108.q = bf16[128,2048]{1,0:T(8,128)(2,1)} reshape(bf16[32,4,2048]{2,1,0:T(4,128)(2,1)} %get-tuple-element.8) | data formatting | bytes 1048576 | tf_op jit(solution)/shard_map/reshape | solution.py:596
  32.5 0.7 fusion.6
  33.3 0.9 copy.38
  34.9 0.2 broadcast_in_dim.75
  35.1 0.7 fusion.5
  35.8 1.4 dynamic-slice_convert_fusion
  37.3 0.1 copy.41
  37.5 0.1 compare_reduce_fusion
  37.6 0.2 copy.40
  37.8 0.1 fusion.4
  37.9 0.1 copy.39
  38.2 0.7 fusion
  38.9 0.8 copy.42.sel
  39.7 155.2 %layer.1 = (bf16[32,4,128]{2,1,0:T(4,128)(2,1)}, bf16[4,4096]{1,0:T(4,128)(2,1)}) custom-call(bf16[128,2048]{1,0:T(8,128)(2,1)} %reshape.108.q, bf16[1056,128]{1,0:T(8,128)(2,1)} %bitcast.47, bf16[128,1056]{1,0:T(8,128)(2,1)} %bitcast.46, f32[1056,128]{1,0:T(8,128)} %bitcast.44, bf16[128,128]{1,0:T(8,128)(2,1)} %bitcast.57, bf16[128,4096]{1,0:T(8,128)(2,1)} %w_out.1, ...), custom_call_target="tpu_custom_call" | custom-call | tf_op jit(solution)/shard_map/layer/pallas_call | solution.py:620
  194.9 0.8 copy.43
  195.7 0.6 reshape.114
  196.3 1.4 copy.50
  (30 shorter events, 0.5 us)
Async XLA Ops:
  2.6 1.4 copy-start.2
  2.7 2.0 %copy-start.5 = (s32[1,128]{1,0:T(1,128)S(1)}, s32[1,128]{1,0:T(1,128)}, u32[]{:S(2)}) copy-start(s32[1,128]{1,0:T(1,128)} %param.17) | copy-start | bytes 1540
  30.5 2.0 %copy-start.1 = (bf16[2,2,528,128]{3,2,1,0:T(8,128)(2,1)S(1)}, bf16[2,2,528,128]{3,2,1,0:T(8,128)(2,1)}, u32[]{:S(2)}) copy-start(bf16[2,2,528,128]{3,2,1,0:T(8,128)(2,1)} %get-tuple-element.9) | copy-start | bytes 1622020
  32.5 4.7 %copy-start.4 = (bf16[1,128,8]{1,2,0:T(8,128)(2,1)S(1)}, bf16[1,128,8]{1,2,0:T(8,128)(2,1)}, u32[]{:S(2)}) copy-start(bf16[1,128,8]{1,2,0:T(8,128)(2,1)} %param.22) | copy-start | bytes 6148
  32.5 4.7 %copy-start.3 = (s32[1,128,8]{1,2,0:T(8,128)S(1)}, s32[1,128,8]{1,2,0:T(8,128)}, u32[]{:S(2)}) copy-start(s32[1,128,8]{1,2,0:T(8,128)} %param.21) | copy-start | bytes 12292
  35.8 3.1 %copy-start = (f32[2,528,128]{2,1,0:T(8,128)}, f32[2,528,128]{2,1,0:T(8,128)S(1)}, u32[]{:S(2)}) copy-start(f32[2,528,128]{2,1,0:T(8,128)S(1)} %constant_dynamic-update-slice_fusion) | copy-start | bytes 1622020

commit v2 on v1

v2 whole, which is shorter than its diff:
```python
import jax
import jax.numpy as jnp
from jax import lax
from jax.experimental import pallas as pl
from jax.experimental.pallas import tpu as pltpu
from jax.sharding import PartitionSpec as P

BF = jnp.bfloat16
F32 = jnp.float32
MESH = pl.DeviceIdType.MESH
NX, NY = 4, 8
NR, NS = 16, 32
SPAN = 528
KEYS = 2 * SPAN
CHUNKS = 4
MASKED = -1e30
FLOOR = -1e29
EPS = 1e-06


def rem(a, b):
    return lax.rem(a, jnp.int32(b))


def div(a, b):
    return lax.div(a, jnp.int32(b))


def place():
    r = lax.axis_index("req")
    s = lax.axis_index("seq")
    return r, s, rem(s, NX), div(s, NX)


def remote(src, dst, send, recv, r, s):
    return pltpu.make_async_remote_copy(
        src_ref=src, dst_ref=dst, send_sem=send, recv_sem=recv, device_id=(r, s), device_id_type=MESH
    )


def loop(n, first=0):
    def run(fn):
        def step(i, c):
            fn(i)
            return c

        lax.fori_loop(first, n, step, 0)

    return run


def dot(a, b):
    return jnp.dot(a, b, preferred_element_type=F32)


def reach_of(o):
    half = div(o + 1, 2)
    return jnp.where(rem(o, 2) == 1, half, rem(NR - half, NR))


def lanes(first, size):
    return pl.ds(pl.multiple_of(first, 128), size)


def part_of(g):
    return slice(128 * g, 128 * g + 128)


def layer_kernel(
    q, k_in, vt_in, res, link, length, ids, gates, gain, w_out, w_gate, w_up, w_down,
    a_out, e_out,
    qy, q_got, qf, k, vt, bias, res_got, rf, reach, reach_f, chosen, rates, sel, back,
    out_src, st_src, got, got_st, p_src, p_got, y_src, y_got, a_src, sq_src, sq, mid_src, mid_q,
    d_src, rows, wgu, wd, gu_src, gu, hid_src, hid, pair_src, pair, ret_src, ret, f_src, fin,
    qys, qyr, qxs, qxr, ks, kr, rs, rr,
    hs, hr, ts, tr, ps, pr, ys, yr, as_, ar, qs, qr, ms, mr, zs, zr, fs, fr,
    gs, gr, us, ur, ds_, dr, gus, gur, hds, hdr, pas, par, bs, br, es, er, ls,
):
    r, s, x, y = place()
    h = rem(x, 2)
    b = rem(y, 2)
    j = div(y, 2)
    top = div(y, 4)
    mate = s + NX - 2 * NX * b
    twin = s + 1 - 2 * h
    number = y * 2 + div(x, 2)
    barrier = pltpu.get_barrier_semaphore()

    @loop(NS, 1)
    def _(d):
        pl.semaphore_signal(barrier, inc=1, device_id=(r, rem(s + d, NS)), device_id_type=MESH)

    @loop(NR, 1)
    def _(d):
        pl.semaphore_signal(barrier, inc=1, device_id=(rem(r + d, NR), s), device_id_type=MESH)

    def x_at(e):
        return rem(x + e, NX)

    def gate_copy(e, first=0, size=1024):
        to = x_at(e)
        span = pl.ds(first, size)
        return remote(w_gate.at[to, span], wgu.at[x, span, pl.ds(0, 128)], gs.at[e], gr.at[e], r, y * NX + to)

    def up_copy(e):
        to = x_at(e)
        return remote(w_up.at[to], wgu.at[x, :, pl.ds(128, 128)], us.at[e], ur.at[e], r, y * NX + to)

    def down_copy(e):
        to = x_at(e)
        return remote(w_down.at[:, lanes(to * 1024, 1024)], wd.at[x], ds_.at[e], dr.at[e], r, y * NX + to)

    own_g = pltpu.make_async_copy(w_gate.at[x], wgu.at[x, :, pl.ds(0, 128)], ls.at[0])
    own_u = pltpu.make_async_copy(w_up.at[x], wgu.at[x, :, pl.ds(128, 128)], ls.at[1])
    own_d = pltpu.make_async_copy(w_down.at[:, lanes(x * 1024, 1024)], wd.at[x], ls.at[2])
    own_g.start()
    own_u.start()
    own_d.start()

    def qy_copy(d):
        return remote(q, qy.at[y], qys.at[d], qyr.at[d], r, rem(y + d, NY) * NX + x)

    def qx_copy(d, e):
        row = rem(y + NY - d, NY)
        to = x_at(e)
        cols = lanes(rem(to, 2) * 2048, 2048)
        return remote(qy.at[row, :, cols], q_got.at[row * NX + x], qxs.at[d, e], qxr.at[d, e], r, y * NX + to)

    def first_copy(e):
        to = x_at(e)
        cols = lanes(rem(to, 2) * 2048, 2048)
        return remote(q.at[:, cols], q_got.at[y * NX + x], qxs.at[0, e], qxr.at[0, e], r, y * NX + to)

    def k_copy():
        return remote(k_in.at[1 - h], k.at[h], ks.at[0], kr.at[0], r, twin)

    def v_copy():
        return remote(vt_in.at[1 - h], vt.at[h], ks.at[1], kr.at[1], r, twin)

    def column(to):
        return lanes(rem(to, NX) * 1024 + div(to, NX) * 128, 128)

    def res_copy(d):
        to = rem(s + d, NS)
        return remote(res.at[:, column(to)], res_got.at[s], rs.at[d], rr.at[d], r, to)

    pl.semaphore_wait(barrier, NS + NR - 2)

    @loop(NY, 1)
    def _(d):
        qy_copy(d).start()

    for e in (2, 1, 3):
        first_copy(e).start()
    k_copy().start()
    v_copy().start()
    mine_q = lanes(h * 2048, 2048)
    q_got[s] = q[:, mine_q]
    k[h] = k_in[h]
    vt[h] = vt_in[h]
    res_got[s] = res[:, column(s)]

    for o in range(NR):
        expert = (4 * rem(r + reach_of(jnp.int32(o)), NR) + j).astype(F32)
        hit = ids[...] == expert
        chosen[o : o + 1, :] = jnp.sum(jnp.where(hit, 1.0, 0.0), axis=0, keepdims=True)
        rates[o : o + 1, :] = jnp.sum(jnp.where(hit, gates[...], 0.0), axis=0, keepdims=True)

    @loop(NY, 1)
    def _(d):
        qy_copy(d).wait_recv()
        for e in (2, 1, 3):
            qx_copy(d, e).start()
        row = rem(y + NY - d, NY)
        q_got[row * NX + x] = qy[row, :, mine_q]

    @loop(NS, 1)
    def _(d):
        res_copy(d).start()

    reach[...] = link[...]

    @loop(5)
    def _(i):
        reach[...] = jnp.minimum(dot(reach[...], reach[...]), 1.0).astype(BF)

    reach_f[...] = jnp.where(reach[...].astype(F32) > 0.5, 0.0, MASKED)
    kin = reach_f[pl.ds(pl.multiple_of(8 * div(s, 2), 8), 8), :]
    spot = lax.broadcasted_iota(jnp.int32, (SPAN, 128), 0)
    for p in range(2):
        first = ((s - h + p) * 512).astype(F32)
        seen = (spot < 512) & (spot.astype(F32) + first < length[...])
        bias[p * SPAN : (p + 1) * SPAN, :] = jnp.where(seen, 0.0, MASKED)
        bias[p * SPAN + 512 : p * SPAN + 516, :] = kin[4 * p : 4 * p + 4, :]

    earlier = lax.broadcasted_iota(jnp.int32, (128, 128), 0) < lax.broadcasted_iota(jnp.int32, (128, 128), 1)
    slot = dot(chosen[...].astype(BF), jnp.where(earlier, 1.0, 0.0).astype(BF))
    seat = lax.broadcasted_iota(jnp.int32, (32, 128), 0).astype(F32)
    for g in range(CHUNKS):
        tall = []
        for o in range(4 * g, 4 * g + 4):
            hit = (slot[o : o + 1, :] == seat) & (chosen[o : o + 1, :] > 0.5)
            tall.append(jnp.where(hit, rates[o : o + 1, :], 0.0))
            sel[32 * o : 32 * o + 32, :] = jnp.where(hit, 1.0, 0.0).astype(BF)
        back[:, part_of(g)] = jnp.transpose(jnp.concatenate(tall, axis=0)).astype(BF)

    k_copy().wait()
    v_copy().wait()
    for e in range(1, NX):
        first_copy(e).wait()

    @loop(NY, 1)
    def _(d):
        qy_copy(d).wait_send()
        for e in range(1, NX):
            qx_copy(d, e).wait()

    for t in range(NS):
        qf[4 * t : 4 * t + 4, :] = q_got[t].astype(F32)

    def out_copy(i):
        return remote(out_src.at[i], got.at[number], hs.at[i], hr.at[number], r, 16 * h + i)

    def st_copy(i):
        return remote(st_src.at[i], got_st.at[number], ts.at[i], tr.at[number], r, 16 * h + i)

    def head_at(n):
        return rem(n + number, 16)

    def send_head(i):
        @pl.when(16 * h + i != s)
        def _():
            out_copy(i).start()
            st_copy(i).start()

        @pl.when(16 * h + i == s)
        def _():
            got[number] = out_src[i]
            got_st[number] = st_src[i]

    @loop(16)
    def _(n):
        i = head_at(n)
        heads = qf[:, lanes(i * 128, 128)].astype(BF)
        score = lax.dot_general(
            k[...].reshape(KEYS, 128), heads, (((1,), (1,)), ((), ())), preferred_element_type=F32
        )
        score = score * (128 ** (-0.5)) + bias[...]
        peak = jnp.maximum(jnp.max(score, axis=0, keepdims=True), FLOOR)
        prob = jnp.exp(score - peak)
        total = jnp.sum(prob, axis=0, keepdims=True)
        prob = prob.astype(BF)
        out_src[i] = (dot(vt[0], prob[:SPAN]) + dot(vt[1], prob[SPAN:])).astype(BF)
        st_src[i] = jnp.concatenate([jnp.broadcast_to(peak, (8, 128)), jnp.broadcast_to(total, (8, 128))], axis=0)

        @pl.when(n >= 1)
        def _():
            send_head(head_at(n + 15))

        for e in (1, 3):
            gate_copy(jnp.int32(e), pl.multiple_of(64 * n, 64), 64).start()

    send_head(head_at(jnp.int32(15)))
    gate_copy(jnp.int32(2)).start()

    @loop(NS, 1)
    def _(d):
        res_copy(d).wait()

    for t in range(NS):
        rf[4 * t : 4 * t + 4, :] = res_got[t].astype(F32)

    @loop(16)
    def _(n):
        who = div(n, 2) * NX + 2 * rem(n, 2) + top

        @pl.when(who != s)
        def _():
            remote(out_src.at[0], got.at[n], hs.at[0], hr.at[n], r, who).wait_recv()
            remote(st_src.at[0], got_st.at[n], ts.at[0], tr.at[n], r, who).wait_recv()

    peaks = got_st[:, 0:1, :]
    totals = got_st[:, 8:9, :]
    peak = jnp.max(peaks, axis=0)
    factor = jnp.exp(peaks - peak[None])
    denom = jnp.sum(factor * totals, axis=0)
    numer = jnp.zeros((128, 128), F32)
    for n in range(16):
        numer = numer + factor[n] * got[n].astype(F32)
    att = jnp.transpose(numer / denom).astype(BF)

    def p_copy(e):
        return remote(p_src.at[e], p_got.at[e], ps.at[e], pr.at[e], r, y * NX + x_at(e))

    for e in (2, 1, 3, 0):
        p_src[e] = dot(att, w_out[:, lanes(x_at(jnp.int32(e)) * 1024, 1024)]).astype(BF)
        if e:
            p_copy(e).start()
    for e in (2, 1, 3):
        up_copy(jnp.int32(e)).start()
    for e in (2, 1, 3):
        down_copy(jnp.int32(e)).start()
    for e in range(1, NX):
        p_copy(e).wait_recv()

    def y_copy(d):
        to = rem(y + d, NY)
        return remote(y_src.at[to], y_got.at[d], ys.at[d], yr.at[d], r, to * NX + x)

    for t in range(NY):
        acc = p_src[0, :, part_of(t)].astype(F32)
        for e in range(1, NX):
            acc = acc + p_got[e, :, part_of(t)].astype(F32)
        y_src[t] = acc.astype(BF)

    @loop(NY, 1)
    def _(d):
        y_copy(d).start()

    acc = y_src[y].astype(F32)
    for d in range(1, NY):
        y_copy(jnp.int32(d)).wait_recv()
        acc = acc + y_got[d].astype(F32)
    attended = acc.astype(BF)
    wide = attended.astype(F32)
    mid = (rf[...] + wide).astype(BF)
    midf = mid.astype(F32)
    mid_src[...] = mid
    col = jnp.sum(midf * midf, axis=1, keepdims=True)
    sq_src[...] = jnp.transpose(jnp.broadcast_to(col, (128, 128)))[0:8, :]
    sq[s] = sq_src[...]

    def mid_copy(n):
        to = (2 * n + top) * NX + x
        return remote(mid_src, mid_q.at[rem(y, 4)], ms.at[n], mr.at[rem(y, 4)], r, to)

    def sq_copy(d):
        return remote(sq_src, sq.at[s], qs.at[d], qr.at[d], r, rem(s + d, NS))

    def a_copy(d):
        to = rem(s + d, NS)
        return remote(a_src.at[to], a_out.at[:, column(s)], as_.at[d], ar.at[d], r, to)

    @loop(NS, 1)
    def _(d):
        sq_copy(d).start()

    @loop(4)
    def _(n):
        @pl.when(2 * n + top != y)
        def _():
            mid_copy(n).start()

        @pl.when(2 * n + top == y)
        def _():
            mid_q[rem(y, 4)] = mid_src[...]

    for t in range(NS):
        a_src[t] = wide[4 * t : 4 * t + 4, :].astype(BF)
    a_out[:, column(s)] = a_src[s]

    @loop(NS, 1)
    def _(d):
        a_copy(d).start()

    @loop(4)
    def _(t):
        @pl.when(4 * b + t != y)
        def _():
            remote(mid_src, mid_q.at[t], ms.at[0], mr.at[t], r, (4 * b + t) * NX + x).wait_recv()

    @loop(NS, 1)
    def _(d):
        sq_copy(d).wait_recv()

    square = jnp.sum(sq[:, 0:1, :], axis=0)
    scale = lax.rsqrt(square * (1.0 / 4096.0) + EPS)
    scale = jnp.transpose(jnp.broadcast_to(scale, (128, 128)))
    half = x * 2 + b

    def z_copy(o):
        to = rem(r + reach_of(o), NR)
        return remote(d_src.at[o], rows.at[b, o], zs.at[o], zr.at[o], to, s)

    def pass_copy(o):
        return remote(rows.at[b, o], rows.at[b, o], fs.at[o], fr.at[o], r, mate)

    def pass_got(o):
        return remote(rows.at[1 - b, o], rows.at[1 - b, o], fs.at[o], fr.at[o], r, mate)

    normed = jnp.concatenate(
        [(mid_q[t].astype(F32) * scale * gain[half, t]).astype(BF) for t in range(4)], axis=1
    )
    for g in range(CHUNKS):
        d_src[4 * g : 4 * g + 4] = dot(sel[part_of(g), :], normed).astype(BF).reshape(4, 32, 512)
        for o in range(max(4 * g, 1), 4 * g + 4):
            z_copy(jnp.int32(o)).start()
    rows[b, 0] = d_src[0]
    pass_copy(jnp.int32(0)).start()

    def gu_copy(e, g):
        return remote(
            gu_src.at[e, pl.ds(128 * g, 128)], gu.at[e, pl.ds(128 * g, 128)], gus.at[e, g], gur.at[e, g],
            r, y * NX + x_at(e),
        )

    def hid_copy(e, g):
        return remote(
            hid_src.at[pl.ds(128 * g, 128)], hid.at[x, pl.ds(128 * g, 128)], hds.at[e, g], hdr.at[e, g],
            r, y * NX + x_at(e),
        )

    def pair_copy(g):
        span = pl.ds(128 * g, 128)
        return remote(pair_src.at[span], pair.at[span], pas.at[g], par.at[g], r, mate)

    def b_copy(o):
        to = rem(r + NR - reach_of(o), NR)
        return remote(ret_src.at[o], ret.at[o], bs.at[o], br.at[o], to, s)

    def forward(g):
        for o in range(max(4 * g, 1), 4 * g + 4):
            z_copy(jnp.int32(o)).wait_recv()
            pass_copy(jnp.int32(o)).start()

    def gate_up(g):
        if g == 0:
            own_g.wait()
            own_u.wait()
            for e in range(1, NX):
                gate_copy(jnp.int32(e)).wait()
                up_copy(jnp.int32(e)).wait()
        for o in range(4 * g, 4 * g + 4):
            pass_got(jnp.int32(o)).wait_recv()
        left = rows[0, 4 * g : 4 * g + 4].reshape(128, 512)
        right = rows[1, 4 * g : 4 * g + 4].reshape(128, 512)
        for e in (2, 1, 3, 0):
            to = x_at(jnp.int32(e))
            gu_src[e, part_of(g), :] = (dot(left, wgu[to, 0:512, :]) + dot(right, wgu[to, 512:1024, :])).astype(BF)
            if e:
                gu_copy(e, g).start()

    def hidden(g):
        acc = gu_src[0, part_of(g), :].astype(F32)
        for e in range(1, NX):
            gu_copy(e, g).wait_recv()
            acc = acc + gu[e, part_of(g), :].astype(F32)
        gate = acc[:, 0:128]
        hid_src[part_of(g), :] = (gate / (1.0 + jnp.exp(-gate)) * acc[:, 128:256]).astype(BF)
        for e in (2, 1, 3):
            hid_copy(e, g).start()
        hid[x, part_of(g), :] = hid_src[part_of(g), :]

    def product(g, side):
        cols = lanes(side * 512, 512)
        acc = dot(hid[0, part_of(g), :], wd[0, :, cols])
        for t in range(1, NX):
            acc = acc + dot(hid[t, part_of(g), :], wd[t, :, cols])
        return acc

    def down(g):
        if g == 0:
            own_d.wait()
            for e in range(1, NX):
                down_copy(jnp.int32(e)).wait()
        for e in range(1, NX):
            hid_copy(e, g).wait_recv()
        pair_src[part_of(g), :] = product(g, 1 - b).astype(BF)
        pair_copy(g).start()

    def give(g):
        acc = product(g, b)
        pair_copy(g).wait_recv()
        acc = acc + pair[part_of(g), :].astype(F32)
        ret_src[4 * g : 4 * g + 4] = acc.astype(BF).reshape(4, 32, 512)
        for o in range(max(4 * g, 1), 4 * g + 4):
            b_copy(jnp.int32(o)).start()
        if g == 0:
            ret[0] = ret_src[0]

    forward(0)
    forward(1)
    gate_up(0)
    forward(2)
    gate_up(1)
    forward(3)
    gate_up(2)
    hidden(0)
    gate_up(3)
    hidden(1)
    down(0)
    hidden(2)
    down(1)
    give(0)
    hidden(3)
    down(2)
    give(1)
    down(3)
    give(2)
    give(3)

    total = jnp.zeros((128, 512), F32)
    for g in range(CHUNKS):
        for o in range(max(4 * g, 1), 4 * g + 4):
            b_copy(jnp.int32(o)).wait_recv()
        total = total + dot(back[:, part_of(g)], ret[4 * g : 4 * g + 4].reshape(128, 512))
    for t in range(NS):
        f_src[t] = total[4 * t : 4 * t + 4, :].astype(BF)

    def f_copy(d):
        to = rem(s + d, NS)
        return remote(f_src.at[to], fin.at[s], es.at[d], er.at[d], r, to)

    fin[s] = f_src[s]

    @loop(NS, 1)
    def _(d):
        f_copy(d).start()

    @loop(16)
    def _(i):
        @pl.when(16 * h + i != s)
        def _():
            out_copy(i).wait_send()
            st_copy(i).wait_send()

    for e in range(1, NX):
        p_copy(e).wait_send()
        for g in range(CHUNKS):
            gu_copy(e, g).wait_send()
            hid_copy(e, g).wait_send()

    @loop(NY, 1)
    def _(d):
        y_copy(d).wait_send()

    @loop(4)
    def _(n):
        @pl.when(2 * n + top != y)
        def _():
            mid_copy(n).wait_send()

    @loop(NS, 1)
    def _(d):
        sq_copy(d).wait_send()
        a_copy(d).wait()

    @loop(NR, 1)
    def _(o):
        z_copy(o).wait_send()
        b_copy(o).wait_send()

    @loop(NR)
    def _(o):
        pass_copy(o).wait_send()

    for g in range(CHUNKS):
        pair_copy(g).wait_send()

    @loop(NS, 1)
    def _(d):
        f_copy(d).wait()

    for xx in range(NX):
        for bb in range(2):
            acc = fin[bb * NX + xx].astype(F32)
            for n in range(1, 4):
                acc = acc + fin[(2 * n + bb) * NX + xx].astype(F32)
            e_out[:, 1024 * xx + 512 * bb : 1024 * xx + 512 * bb + 512] = acc.astype(BF)


VM = pl.BlockSpec(memory_space=pltpu.VMEM)
HB = pl.BlockSpec(memory_space=pl.ANY)


def sds(shape, dtype=BF):
    return jax.ShapeDtypeStruct(shape, dtype)


def dma(*shape):
    return pltpu.SemaphoreType.DMA(shape)


def vm(*shape, dtype=BF):
    return pltpu.VMEM(shape, dtype)


def body(
    queries, kv_cache, tree_kv, context_lengths, tree_parents, resid, out_weight, norm_gain,
    expert_ids, gate_weights, w_gate, w_up, w_down,
):
    both = jnp.concatenate([kv_cache[0], tree_kv[0], jnp.zeros((12, 2, 256), BF)], axis=0)
    k_in = both[:, 0].reshape(SPAN, 2, 128).transpose(1, 0, 2)
    vt_in = both[:, 1].reshape(SPAN, 2, 128).transpose(1, 2, 0)
    parents = tree_parents[0]
    node = jnp.arange(128, dtype=jnp.int32)
    link = ((parents[None, :] == node[:, None]) | (node[:, None] == node[None, :])).astype(BF)
    length = jnp.broadcast_to(context_lengths.astype(F32)[:, None], (1, 128))
    gain = norm_gain.astype(F32).reshape(8, 4, 1, 128)
    a_out, e_out = pl.pallas_call(
        layer_kernel,
        name="layer",
        out_shape=(sds((4, 4096)), sds((4, 4096))),
        in_specs=[VM] * 10 + [HB] * 3,
        out_specs=(VM, VM),
        scratch_shapes=[
            vm(NY, 4, 4096), vm(NS, 4, 2048), vm(128, 2048, dtype=F32), vm(2, SPAN, 128), vm(2, 128, SPAN),
            vm(KEYS, 128, dtype=F32), vm(NS, 4, 128), vm(128, 128, dtype=F32), vm(128, 128),
            vm(128, 128, dtype=F32), vm(NR, 128, dtype=F32), vm(NR, 128, dtype=F32), vm(512, 128), vm(128, 512),
            vm(16, 128, 128), vm(16, 16, 128, dtype=F32), vm(16, 128, 128), vm(16, 16, 128, dtype=F32),
            vm(NX, 128, 1024), vm(NX, 128, 1024), vm(NY, 128, 128), vm(NY, 128, 128),
            vm(NS, 4, 128), vm(8, 128, dtype=F32), vm(NS, 8, 128, dtype=F32), vm(128, 128), vm(4, 128, 128),
            vm(16, 32, 512), vm(2, 16, 32, 512), vm(NX, 1024, 256), vm(NX, 128, 1024),
            vm(NX, 512, 256), vm(NX, 512, 256), vm(512, 128), vm(NX, 512, 128), vm(512, 512), vm(512, 512),
            vm(16, 32, 512), vm(16, 32, 512), vm(NS, 4, 512), vm(NS, 4, 512),
            dma(NY), dma(NY), dma(NY, NX), dma(NY, NX), dma(2), dma(2), dma(NS), dma(NS),
            dma(16), dma(16), dma(16), dma(16), dma(4), dma(4), dma(NY), dma(NY),
            dma(NS), dma(NS), dma(NS), dma(NS), dma(4), dma(4), dma(NR), dma(NR), dma(NR), dma(NR),
            dma(4), dma(4), dma(4), dma(4), dma(4), dma(4), dma(NX, CHUNKS), dma(NX, CHUNKS),
            dma(NX, CHUNKS), dma(NX, CHUNKS), dma(CHUNKS), dma(CHUNKS), dma(NR), dma(NR), dma(NS), dma(NS), dma(3),
        ],
        compiler_params=pltpu.CompilerParams(collective_id=0, has_side_effects=True),
    )(
        queries[0], k_in, vt_in, resid[0], link, length,
        expert_ids[0].T.astype(F32), gate_weights[0].T.astype(F32), gain, out_weight,
        w_gate[0].reshape(NX, 1024, 128), w_up[0].reshape(NX, 1024, 128), w_down[0],
    )
    return a_out[None], e_out[None]


def solution(mesh):
    placed = (
        P("req", "seq", None),
        P("req", "seq", None, None),
        P("req", "seq", None, None),
        P("req"),
        P("req", None),
        P("req", "seq", None),
        P("seq", None),
        P(),
        P("req", None, None),
        P("req", None, None),
        P(("req", "seq"), None, None),
        P(("req", "seq"), None, None),
        P(("req", "seq"), None, None),
    )
    return jax.shard_map(
        body,
        mesh=mesh,
        in_specs=placed,
        out_specs=(P("req", "seq", None), P("req", "seq", None)),
        check_vma=False,
    )
```

time: 200 us -> 177 us (0.89)
  Pallas kernels: 180 us -> 160 us
  local copies, waits for them, and re-layouts: 11 us -> 7.94 us
  other arithmetic: 4.74 us -> 7 us
    pallas_call x2 -> x1, Pallas kernels: 180 us -> 160 us  [body(): pl.pallas_call(layer_kernel, name='layer', out_shape=(sds((4, 4096)), sds...]
    concatenate x0 -> x1, other arithmetic: none -> 4.58 us  [body(): jnp.concatenate([kv_cache[0], tree_kv[0], jnp.zeros((12, 2, 256), BF)], a...]
    reshape x2 -> x0, local copies, waits for them, and re-layouts: 2.64 us -> none  [the longest x1 2.01 us: body(): query = q_out.reshape(128, 2048)]
    slice x1 -> x2, local copies, waits for them, and re-layouts: 0.73 us -> 3.24 us  [body(): vt_in = both[:, 1].reshape(SPAN, 2, 128).transpose(1, 2, 0)]
where the time goes in v2:
time: 177 us
  Pallas kernels  160 us (90%)
  local copies, waits for them, and re-layouts  7.94 us (4%)
  other arithmetic  7 us (4%)
    pallas_call x1, Pallas kernels, body(): pl.pallas_call(layer_kernel, name='layer', out_shape=(sds((4, 4096)), sds...  160 us
    concatenate x1, other arithmetic, body(): jnp.concatenate([kv_cache[0], tree_kv[0], jnp.zeros((12, 2, 256), BF)], a...  4.58 us

profile of v2, /device:TPU:1, one launch (start us, length us, event | category | flops | bytes accessed | tf_op | source)
XLA Modules:
  0.0 176.6 jit_solution(10544636100081887111)
XLA Ops:
  0.6 0.0 copy-start.2
  0.7 0.1 pad.2.clone
  0.7 0.6 copy-done.2
  1.3 4.6 %maximum_maximum_fusion = bf16[528,2,256]{2,1,0:T(2,128)(2,1)S(1)} fusion(bf16[4,2,256]{2,1,0:T(2,128)(2,1)S(1)} %bitcast.41, bf16[512,2,256]{2,1,0:T(2,128)(2,1)} %bitcast.35, bf16[528]{0:T(1024)(128)(2,1)S(1)} %pad.2.clone), kind=kLoop, calls=%fused_computation.1 | loop fusion | flops 540672 | bytes 1070112 | tf_op jit(solution)/shard_map/concatenate | solution.py:592
  5.9 1.9 %fusion.2 = (bf16[528,1,256]{2,1,0:T(2,128)(2,1)S(1)}, bf16[528,256]{1,0:T(8,128)(2,1)S(1)}) fusion(bf16[528,2,256]{2,1,0:T(2,128)(2,1)S(1)} %maximum_maximum_fusion), kind=kLoop, calls=%fused_computation.9 | loop fusion | bytes 1081344 | tf_op jit(solution)/shard_map/slice | solution.py:594
  7.8 1.4 copy.17
  9.2 0.7 bitcast_bitcast_fusion.k_in
  9.9 0.0 copy-start.5
  9.9 0.7 copy-done.5
  10.5 0.0 copy-start.1
  10.5 0.0 copy-start.4
  10.5 0.6 fusion.1.link
  11.2 0.1 copy-done.1
  11.2 0.6 reshape.17
  11.8 0.0 copy-done.4
  11.8 0.6 convert_bitcast_fusion.gates
  12.4 0.1 copy-done.3
  12.5 0.6 convert_bitcast_fusion.1.ids
  13.8 0.5 broadcast_in_dim.22.length
  14.3 160.3 %layer.1 = (bf16[4,4096]{1,0:T(4,128)(2,1)}, bf16[4,4096]{1,0:T(4,128)(2,1)}) custom-call(bf16[4,4096]{1,0:T(4,128)(2,1)} %bitcast.37, bf16[2,528,128]{2,1,0:T(8,128)(2,1)} %bitcast_bitcast_fusion.k_in, bf16[2,128,528]{2,1,0:T(8,128)(2,1)} %bitcast.31, bf16[4,4096]{1,0:T(4,128)(2,1)} %bitcast.38, bf16[128,128]{1,0:T(8,128)(2,1)} %fusion.1.link, ...), custom_call_target="tpu_custom_call" | custom-call | tf_op jit(solution)/shard_map/layer/pallas_call | solution.py:600
  174.5 0.0 copy-start
  174.5 1.4 copy.23
  175.9 0.0 copy-done
  175.9 0.6 copy.24
  (2 shorter events, 0.0 us)
Async XLA Ops:
  0.6 0.7 copy-start.2
  9.9 0.7 copy-start.5
  10.5 0.7 copy-start.1
  10.5 1.3 copy-start.4
  11.8 0.7 copy-start.3
  174.5 1.4 copy-start

commit v3 on v2

--- a/solution.py
+++ b/solution.py
@@ -53,9 +53,17 @@
     return jnp.dot(a, b, preferred_element_type=F32)
 
 
+def spread_of(o, n):
+    o = n - 1 - o
+    half = div(o + 1, 2)
+    return jnp.where(rem(o, 2) == 1, half, rem(n - half, n))
+
+
 def reach_of(o):
-    half = div(o + 1, 2)
-    return jnp.where(rem(o, 2) == 1, half, rem(NR - half, NR))
+    return spread_of(o, NR)
+
+
+FAR = (4, 3, 5, 2, 6, 1, 7, 0)
 
 
 def lanes(first, size):
@@ -67,9 +75,9 @@
 
 
 def layer_kernel(
-    q, k_in, vt_in, res, link, length, ids, gates, gain, w_out, w_gate, w_up, w_down,
+    q, kv_in, tree_in, res, parents, length, ids, gates, gain, w_out, w_gate, w_up, w_down,
     a_out, e_out,
-    qy, q_got, qf, k, vt, bias, res_got, rf, reach, reach_f, chosen, rates, sel, back,
+    qy, q_got, qf, k, v, vt, bias, res_got, rf, reach, reach_f, chosen, rates, sel, back,
     out_src, st_src, got, got_st, p_src, p_got, y_src, y_got, a_src, sq_src, sq, mid_src, mid_q,
     d_src, rows, wgu, wd, gu_src, gu, hid_src, hid, pair_src, pair, ret_src, ret, f_src, fin,
     qys, qyr, qxs, qxr, ks, kr, rs, rr,
@@ -118,10 +126,10 @@
     own_d.start()
 
     def qy_copy(d):
-        return remote(q, qy.at[y], qys.at[d], qyr.at[d], r, rem(y + d, NY) * NX + x)
+        return remote(q, qy.at[y], qys.at[d], qyr.at[d], r, rem(y + spread_of(d, NY), NY) * NX + x)
 
     def qx_copy(d, e):
-        row = rem(y + NY - d, NY)
+        row = rem(y + NY - spread_of(d, NY), NY)
         to = x_at(e)
         cols = lanes(rem(to, 2) * 2048, 2048)
         return remote(qy.at[row, :, cols], q_got.at[row * NX + x], qxs.at[d, e], qxr.at[d, e], r, y * NX + to)
@@ -129,56 +137,62 @@
     def first_copy(e):
         to = x_at(e)
         cols = lanes(rem(to, 2) * 2048, 2048)
-        return remote(q.at[:, cols], q_got.at[y * NX + x], qxs.at[0, e], qxr.at[0, e], r, y * NX + to)
-
-    def k_copy():
-        return remote(k_in.at[1 - h], k.at[h], ks.at[0], kr.at[0], r, twin)
-
-    def v_copy():
-        return remote(vt_in.at[1 - h], vt.at[h], ks.at[1], kr.at[1], r, twin)
+        return remote(q.at[:, cols], q_got.at[y * NX + x], qxs.at[NY - 1, e], qxr.at[NY - 1, e], r, y * NX + to)
+
+    def kv_copies():
+        ctx, new = pl.ds(0, 512), pl.ds(512, 16)
+        return (
+            remote(kv_in.at[1 - h], k.at[h, ctx], ks.at[0], kr.at[0], r, twin),
+            remote(kv_in.at[3 - h], v.at[h, ctx], ks.at[1], kr.at[1], r, twin),
+            remote(tree_in.at[1 - h], k.at[h, new], ks.at[2], kr.at[2], r, twin),
+            remote(tree_in.at[3 - h], v.at[h, new], ks.at[3], kr.at[3], r, twin),
+        )
 
     def column(to):
         return lanes(rem(to, NX) * 1024 + div(to, NX) * 128, 128)
 
     def res_copy(d):
-        to = rem(s + d, NS)
+        to = rem(s + spread_of(d, NS), NS)
         return remote(res.at[:, column(to)], res_got.at[s], rs.at[d], rr.at[d], r, to)
 
     pl.semaphore_wait(barrier, NS + NR - 2)
 
-    @loop(NY, 1)
+    @loop(NY - 1)
     def _(d):
         qy_copy(d).start()
 
     for e in (2, 1, 3):
         first_copy(e).start()
-    k_copy().start()
-    v_copy().start()
+    for copy in kv_copies():
+        copy.start()
     mine_q = lanes(h * 2048, 2048)
     q_got[s] = q[:, mine_q]
-    k[h] = k_in[h]
-    vt[h] = vt_in[h]
+    k[h, 0:512] = kv_in[h]
+    k[h, 512:528] = tree_in[h]
+    v[h, 0:512] = kv_in[2 + h]
+    v[h, 512:528] = tree_in[2 + h]
     res_got[s] = res[:, column(s)]
 
     for o in range(NR):
-        expert = (4 * rem(r + reach_of(jnp.int32(o)), NR) + j).astype(F32)
-        hit = ids[...] == expert
+        hit = ids[...] == 4 * rem(r + reach_of(jnp.int32(o)), NR) + j
         chosen[o : o + 1, :] = jnp.sum(jnp.where(hit, 1.0, 0.0), axis=0, keepdims=True)
-        rates[o : o + 1, :] = jnp.sum(jnp.where(hit, gates[...], 0.0), axis=0, keepdims=True)
-
-    @loop(NY, 1)
+        rates[o : o + 1, :] = jnp.sum(jnp.where(hit, gates[...].astype(F32), 0.0), axis=0, keepdims=True)
+
+    @loop(NY - 1)
     def _(d):
         qy_copy(d).wait_recv()
         for e in (2, 1, 3):
             qx_copy(d, e).start()
-        row = rem(y + NY - d, NY)
+        row = rem(y + NY - spread_of(d, NY), NY)
         q_got[row * NX + x] = qy[row, :, mine_q]
 
-    @loop(NS, 1)
+    @loop(NS - 1)
     def _(d):
         res_copy(d).start()
 
-    reach[...] = link[...]
+    node = lax.broadcasted_iota(jnp.int32, (128, 128), 0)
+    spot = lax.broadcasted_iota(jnp.int32, (128, 128), 1)
+    reach[...] = jnp.where((parents[...] == node) | (node == spot), 1.0, 0.0).astype(BF)
 
     @loop(5)
     def _(i):
@@ -188,8 +202,8 @@
     kin = reach_f[pl.ds(pl.multiple_of(8 * div(s, 2), 8), 8), :]
     spot = lax.broadcasted_iota(jnp.int32, (SPAN, 128), 0)
     for p in range(2):
-        first = ((s - h + p) * 512).astype(F32)
-        seen = (spot < 512) & (spot.astype(F32) + first < length[...])
+        first = (s - h + p) * 512
+        seen = (spot < 512) & (spot + first < length[0])
         bias[p * SPAN : (p + 1) * SPAN, :] = jnp.where(seen, 0.0, MASKED)
         bias[p * SPAN + 512 : p * SPAN + 516, :] = kin[4 * p : 4 * p + 4, :]
 
@@ -204,12 +218,17 @@
             sel[32 * o : 32 * o + 32, :] = jnp.where(hit, 1.0, 0.0).astype(BF)
         back[:, part_of(g)] = jnp.transpose(jnp.concatenate(tall, axis=0)).astype(BF)
 
-    k_copy().wait()
-    v_copy().wait()
+    for copy in kv_copies():
+        copy.wait()
+    for p in range(2):
+        for t in range(4):
+            vt[p, :, part_of(t)] = jnp.transpose(v[p, part_of(t), :].astype(F32)).astype(BF)
+        last = jnp.concatenate([v[p, 512:528, :].astype(F32), jnp.zeros((112, 128), F32)], axis=0)
+        vt[p, :, 512:528] = jnp.transpose(last)[:, 0:16].astype(BF)
     for e in range(1, NX):
         first_copy(e).wait()
 
-    @loop(NY, 1)
+    @loop(NY - 1)
     def _(d):
         qy_copy(d).wait_send()
         for e in range(1, NX):
@@ -251,7 +270,7 @@
         total = jnp.sum(prob, axis=0, keepdims=True)
         prob = prob.astype(BF)
         out_src[i] = (dot(vt[0], prob[:SPAN]) + dot(vt[1], prob[SPAN:])).astype(BF)
-        st_src[i] = jnp.concatenate([jnp.broadcast_to(peak, (8, 128)), jnp.broadcast_to(total, (8, 128))], axis=0)
+        st_src[i] = jnp.concatenate([peak, total], axis=0)
 
         @pl.when(n >= 1)
         def _():
@@ -263,7 +282,7 @@
     send_head(head_at(jnp.int32(15)))
     gate_copy(jnp.int32(2)).start()
 
-    @loop(NS, 1)
+    @loop(NS - 1)
     def _(d):
         res_copy(d).wait()
 
@@ -280,7 +299,7 @@
             remote(st_src.at[0], got_st.at[n], ts.at[0], tr.at[n], r, who).wait_recv()
 
     peaks = got_st[:, 0:1, :]
-    totals = got_st[:, 8:9, :]
+    totals = got_st[:, 1:2, :]
     peak = jnp.max(peaks, axis=0)
     factor = jnp.exp(peaks - peak[None])
     denom = jnp.sum(factor * totals, axis=0)
@@ -289,45 +308,45 @@
         numer = numer + factor[n] * got[n].astype(F32)
     att = jnp.transpose(numer / denom).astype(BF)
 
-    def p_copy(e):
-        return remote(p_src.at[e], p_got.at[e], ps.at[e], pr.at[e], r, y * NX + x_at(e))
-
-    for e in (2, 1, 3, 0):
-        p_src[e] = dot(att, w_out[:, lanes(x_at(jnp.int32(e)) * 1024, 1024)]).astype(BF)
-        if e:
-            p_copy(e).start()
+    def p_copy(e, n):
+        t = rem(y + FAR[n], NY)
+        return remote(p_src.at[e, t], p_got.at[e, t], ps.at[e, n], pr.at[e, n], r, y * NX + x_at(e))
+
+    for n in range(NY):
+        t = rem(y + FAR[n], NY)
+        for e in (2, 1, 3, 0):
+            cols = lanes(x_at(jnp.int32(e)) * 1024 + t * 128, 128)
+            p_src[e, t] = dot(att, w_out[:, cols]).astype(BF)
+            if e:
+                p_copy(e, n).start()
     for e in (2, 1, 3):
         up_copy(jnp.int32(e)).start()
     for e in (2, 1, 3):
         down_copy(jnp.int32(e)).start()
-    for e in range(1, NX):
-        p_copy(e).wait_recv()
-
-    def y_copy(d):
-        to = rem(y + d, NY)
-        return remote(y_src.at[to], y_got.at[d], ys.at[d], yr.at[d], r, to * NX + x)
-
-    for t in range(NY):
-        acc = p_src[0, :, part_of(t)].astype(F32)
+
+    def y_copy(n):
+        to = rem(y + FAR[n], NY)
+        return remote(y_src.at[n], y_got.at[n], ys.at[n], yr.at[n], r, to * NX + x)
+
+    for n in range(NY):
+        t = rem(y + FAR[n], NY)
+        acc = p_src[0, t].astype(F32)
         for e in range(1, NX):
-            acc = acc + p_got[e, :, part_of(t)].astype(F32)
-        y_src[t] = acc.astype(BF)
-
-    @loop(NY, 1)
-    def _(d):
-        y_copy(d).start()
-
-    acc = y_src[y].astype(F32)
-    for d in range(1, NY):
-        y_copy(jnp.int32(d)).wait_recv()
-        acc = acc + y_got[d].astype(F32)
+            p_copy(e, n).wait_recv()
+            acc = acc + p_got[e, t].astype(F32)
+        if FAR[n]:
+            y_src[n] = acc.astype(BF)
+            y_copy(n).start()
+    for n in range(NY - 1):
+        y_copy(n).wait_recv()
+        acc = acc + y_got[n].astype(F32)
     attended = acc.astype(BF)
     wide = attended.astype(F32)
     mid = (rf[...] + wide).astype(BF)
     midf = mid.astype(F32)
     mid_src[...] = mid
     col = jnp.sum(midf * midf, axis=1, keepdims=True)
-    sq_src[...] = jnp.transpose(jnp.broadcast_to(col, (128, 128)))[0:8, :]
+    sq_src[...] = jnp.transpose(jnp.broadcast_to(col, (128, 128)))[0:1, :]
     sq[s] = sq_src[...]
 
     def mid_copy(n):
@@ -335,13 +354,13 @@
         return remote(mid_src, mid_q.at[rem(y, 4)], ms.at[n], mr.at[rem(y, 4)], r, to)
 
     def sq_copy(d):
-        return remote(sq_src, sq.at[s], qs.at[d], qr.at[d], r, rem(s + d, NS))
+        return remote(sq_src, sq.at[s], qs.at[d], qr.at[d], r, rem(s + spread_of(d, NS), NS))
 
     def a_copy(d):
-        to = rem(s + d, NS)
+        to = rem(s + spread_of(d, NS), NS)
         return remote(a_src.at[to], a_out.at[:, column(s)], as_.at[d], ar.at[d], r, to)
 
-    @loop(NS, 1)
+    @loop(NS - 1)
     def _(d):
         sq_copy(d).start()
 
@@ -359,7 +378,7 @@
         a_src[t] = wide[4 * t : 4 * t + 4, :].astype(BF)
     a_out[:, column(s)] = a_src[s]
 
-    @loop(NS, 1)
+    @loop(NS - 1)
     def _(d):
         a_copy(d).start()
 
@@ -369,11 +388,11 @@
         def _():
             remote(mid_src, mid_q.at[t], ms.at[0], mr.at[t], r, (4 * b + t) * NX + x).wait_recv()
 
-    @loop(NS, 1)
+    @loop(NS - 1)
     def _(d):
         sq_copy(d).wait_recv()
 
-    square = jnp.sum(sq[:, 0:1, :], axis=0)
+    square = jnp.sum(sq[...], axis=0)
     scale = lax.rsqrt(square * (1.0 / 4096.0) + EPS)
     scale = jnp.transpose(jnp.broadcast_to(scale, (128, 128)))
     half = x * 2 + b
@@ -389,14 +408,17 @@
         return remote(rows.at[1 - b, o], rows.at[1 - b, o], fs.at[o], fr.at[o], r, mate)
 
     normed = jnp.concatenate(
-        [(mid_q[t].astype(F32) * scale * gain[half, t]).astype(BF) for t in range(4)], axis=1
+        [
+            (mid_q[t].astype(F32) * scale * gain[:, lanes(half * 512 + 128 * t, 128)].astype(F32)).astype(BF)
+            for t in range(4)
+        ], axis=1
     )
     for g in range(CHUNKS):
         d_src[4 * g : 4 * g + 4] = dot(sel[part_of(g), :], normed).astype(BF).reshape(4, 32, 512)
-        for o in range(max(4 * g, 1), 4 * g + 4):
+        for o in range(4 * g, min(4 * g + 4, NR - 1)):
             z_copy(jnp.int32(o)).start()
-    rows[b, 0] = d_src[0]
-    pass_copy(jnp.int32(0)).start()
+    rows[b, NR - 1] = d_src[NR - 1]
+    pass_copy(jnp.int32(NR - 1)).start()
 
     def gu_copy(e, g):
         return remote(
@@ -419,7 +441,7 @@
         return remote(ret_src.at[o], ret.at[o], bs.at[o], br.at[o], to, s)
 
     def forward(g):
-        for o in range(max(4 * g, 1), 4 * g + 4):
+        for o in range(4 * g, min(4 * g + 4, NR - 1)):
             z_copy(jnp.int32(o)).wait_recv()
             pass_copy(jnp.int32(o)).start()
 
@@ -473,10 +495,10 @@
         pair_copy(g).wait_recv()
         acc = acc + pair[part_of(g), :].astype(F32)
         ret_src[4 * g : 4 * g + 4] = acc.astype(BF).reshape(4, 32, 512)
-        for o in range(max(4 * g, 1), 4 * g + 4):
+        for o in range(4 * g, min(4 * g + 4, NR - 1)):
             b_copy(jnp.int32(o)).start()
-        if g == 0:
-            ret[0] = ret_src[0]
+        if g == CHUNKS - 1:
+            ret[NR - 1] = ret_src[NR - 1]
 
     forward(0)
     forward(1)
@@ -501,19 +523,19 @@
 
     total = jnp.zeros((128, 512), F32)
     for g in range(CHUNKS):
-        for o in range(max(4 * g, 1), 4 * g + 4):
+        for o in range(4 * g, min(4 * g + 4, NR - 1)):
             b_copy(jnp.int32(o)).wait_recv()
         total = total + dot(back[:, part_of(g)], ret[4 * g : 4 * g + 4].reshape(128, 512))
     for t in range(NS):
         f_src[t] = total[4 * t : 4 * t + 4, :].astype(BF)
 
     def f_copy(d):
-        to = rem(s + d, NS)
+        to = rem(s + spread_of(d, NS), NS)
         return remote(f_src.at[to], fin.at[s], es.at[d], er.at[d], r, to)
 
     fin[s] = f_src[s]
 
-    @loop(NS, 1)
+    @loop(NS - 1)
     def _(d):
         f_copy(d).start()
 
@@ -525,14 +547,14 @@
             st_copy(i).wait_send()
 
     for e in range(1, NX):
-        p_copy(e).wait_send()
+        for n in range(NY):
+            p_copy(e, n).wait_send()
         for g in range(CHUNKS):
             gu_copy(e, g).wait_send()
             hid_copy(e, g).wait_send()
 
-    @loop(NY, 1)
-    def _(d):
-        y_copy(d).wait_send()
+    for n in range(NY - 1):
+        y_copy(n).wait_send()
 
     @loop(4)
     def _(n):
@@ -540,12 +562,12 @@
         def _():
             mid_copy(n).wait_send()
 
-    @loop(NS, 1)
+    @loop(NS - 1)
     def _(d):
         sq_copy(d).wait_send()
         a_copy(d).wait()
 
-    @loop(NR, 1)
+    @loop(NR - 1)
     def _(o):
         z_copy(o).wait_send()
         b_copy(o).wait_send()
@@ -557,7 +579,7 @@
     for g in range(CHUNKS):
         pair_copy(g).wait_send()
 
-    @loop(NS, 1)
+    @loop(NS - 1)
     def _(d):
         f_copy(d).wait()
 
@@ -589,40 +611,34 @@
     queries, kv_cache, tree_kv, context_lengths, tree_parents, resid, out_weight, norm_gain,
     expert_ids, gate_weights, w_gate, w_up, w_down,
 ):
-    both = jnp.concatenate([kv_cache[0], tree_kv[0], jnp.zeros((12, 2, 256), BF)], axis=0)
-    k_in = both[:, 0].reshape(SPAN, 2, 128).transpose(1, 0, 2)
-    vt_in = both[:, 1].reshape(SPAN, 2, 128).transpose(1, 2, 0)
-    parents = tree_parents[0]
-    node = jnp.arange(128, dtype=jnp.int32)
-    link = ((parents[None, :] == node[:, None]) | (node[:, None] == node[None, :])).astype(BF)
-    length = jnp.broadcast_to(context_lengths.astype(F32)[:, None], (1, 128))
-    gain = norm_gain.astype(F32).reshape(8, 4, 1, 128)
+    kv_in = kv_cache[0].reshape(512, 4, 128).transpose(1, 0, 2)
+    tree_in = jnp.pad(tree_kv[0].reshape(4, 4, 128).transpose(1, 0, 2), ((0, 0), (0, 12), (0, 0)))
     a_out, e_out = pl.pallas_call(
         layer_kernel,
         name="layer",
         out_shape=(sds((4, 4096)), sds((4, 4096))),
-        in_specs=[VM] * 10 + [HB] * 3,
+        in_specs=[VM] * 5 + [pl.BlockSpec(memory_space=pltpu.SMEM)] + [VM] * 4 + [HB] * 3,
         out_specs=(VM, VM),
         scratch_shapes=[
-            vm(NY, 4, 4096), vm(NS, 4, 2048), vm(128, 2048, dtype=F32), vm(2, SPAN, 128), vm(2, 128, SPAN),
+            vm(NY, 4, 4096), vm(NS, 4, 2048), vm(128, 2048, dtype=F32), vm(2, SPAN, 128), vm(2, SPAN, 128), vm(2, 128, SPAN),
             vm(KEYS, 128, dtype=F32), vm(NS, 4, 128), vm(128, 128, dtype=F32), vm(128, 128),
             vm(128, 128, dtype=F32), vm(NR, 128, dtype=F32), vm(NR, 128, dtype=F32), vm(512, 128), vm(128, 512),
-            vm(16, 128, 128), vm(16, 16, 128, dtype=F32), vm(16, 128, 128), vm(16, 16, 128, dtype=F32),
-            vm(NX, 128, 1024), vm(NX, 128, 1024), vm(NY, 128, 128), vm(NY, 128, 128),
-            vm(NS, 4, 128), vm(8, 128, dtype=F32), vm(NS, 8, 128, dtype=F32), vm(128, 128), vm(4, 128, 128),
+            vm(16, 128, 128), vm(16, 2, 128, dtype=F32), vm(16, 128, 128), vm(16, 2, 128, dtype=F32),
+            vm(NX, NY, 128, 128), vm(NX, NY, 128, 128), vm(NY, 128, 128), vm(NY, 128, 128),
+            vm(NS, 4, 128), vm(1, 128, dtype=F32), vm(NS, 1, 128, dtype=F32), vm(128, 128), vm(4, 128, 128),
             vm(16, 32, 512), vm(2, 16, 32, 512), vm(NX, 1024, 256), vm(NX, 128, 1024),
             vm(NX, 512, 256), vm(NX, 512, 256), vm(512, 128), vm(NX, 512, 128), vm(512, 512), vm(512, 512),
             vm(16, 32, 512), vm(16, 32, 512), vm(NS, 4, 512), vm(NS, 4, 512),
-            dma(NY), dma(NY), dma(NY, NX), dma(NY, NX), dma(2), dma(2), dma(NS), dma(NS),
-            dma(16), dma(16), dma(16), dma(16), dma(4), dma(4), dma(NY), dma(NY),
+            dma(NY), dma(NY), dma(NY, NX), dma(NY, NX), dma(4), dma(4), dma(NS), dma(NS),
+            dma(16), dma(16), dma(16), dma(16), dma(NX, NY), dma(NX, NY), dma(NY), dma(NY),
             dma(NS), dma(NS), dma(NS), dma(NS), dma(4), dma(4), dma(NR), dma(NR), dma(NR), dma(NR),
             dma(4), dma(4), dma(4), dma(4), dma(4), dma(4), dma(NX, CHUNKS), dma(NX, CHUNKS),
             dma(NX, CHUNKS), dma(NX, CHUNKS), dma(CHUNKS), dma(CHUNKS), dma(NR), dma(NR), dma(NS), dma(NS), dma(3),
         ],
         compiler_params=pltpu.CompilerParams(collective_id=0, has_side_effects=True),
     )(
-        queries[0], k_in, vt_in, resid[0], link, length,
-        expert_ids[0].T.astype(F32), gate_weights[0].T.astype(F32), gain, out_weight,
+        queries[0], kv_in, tree_in, resid[0], tree_parents, context_lengths,
+        expert_ids[0].T, gate_weights[0].T, norm_gain.reshape(1, 4096), out_weight,
         w_gate[0].reshape(NX, 1024, 128), w_up[0].reshape(NX, 1024, 128), w_down[0],
     )
     return a_out[None], e_out[None]

time: 177 us -> 162 us (0.915)
  other arithmetic: 7 us -> 0 us
  Pallas kernels: 160 us -> 155 us
  local copies, waits for them, and re-layouts: 7.94 us -> 5.65 us
    pallas_call x1, Pallas kernels: 160 us -> 155 us  [body(): pl.pallas_call(layer_kernel, name='layer', out_shape=(sds((4, 4096)), sds...]
    concatenate x1 -> x0, other arithmetic: 4.58 us -> none  [body(): jnp.concatenate([kv_cache[0], tree_kv[0], jnp.zeros((12, 2, 256), BF)], a...]
    slice x2 -> x0, local copies, waits for them, and re-layouts: 3.24 us -> none  [body(): vt_in = both[:, 1].reshape(SPAN, 2, 128).transpose(1, 2, 0)]
    convert_element_type x3 -> x0, other arithmetic: 1.81 us -> none  [the longest x1 0.63 us: body(): ((parents[None, :] == node[:, None]) | (node[:, None] == node[None, :]))....]
where the time goes in v3:
time: 162 us
  Pallas kernels  155 us (96%)
  local copies, waits for them, and re-layouts  5.65 us (3%)
    pallas_call x1, Pallas kernels, body(): pl.pallas_call(layer_kernel, name='layer', out_shape=(sds((4, 4096)), sds...  155 us
    unnamed x9, local copies, waits for them, and re-layouts  3.41 us

profile of v3, /device:TPU:1, one launch (start us, length us, event | category | flops | bytes accessed | tf_op | source)
XLA Modules:
  0.0 162.0 jit_solution(7429858799438723350)
XLA Ops:
  0.6 1.3 copy.15
  1.9 0.0 copy-start.2
  2.0 1.0 copy.16
  3.0 0.0 copy-done.2
  3.0 0.0 copy-start.1
  3.0 0.6 pad.4.tree_in
  3.6 0.1 copy-done.1
  3.7 0.6 reshape.7.gain
  4.9 155.0 %layer.1 = (bf16[4,4096]{1,0:T(4,128)(2,1)}, bf16[4,4096]{1,0:T(4,128)(2,1)}) custom-call(bf16[4,4096]{1,0:T(4,128)(2,1)} %bitcast.23, bf16[4,512,128]{2,1,0:T(8,128)(2,1)} %bitcast.19, bf16[4,16,128]{2,1,0:T(8,128)(2,1)} %pad.4.tree_in, bf16[4,4096]{1,0:T(4,128)(2,1)} %bitcast.24, s32[1,128]{1,0:T(1,128)} %parents.1, s32[1]{0:T(128)S(6)} %copy.22.length, ...), custom_call_target="tpu_custom_call" | custom-call | tf_op jit(solution)/shard_map/layer/pallas_call | solution.py:616
  160.0 0.0 copy-start
  160.0 1.4 copy.23
  161.4 0.0 copy-done
  161.4 0.6 copy.24
  (2 shorter events, 0.0 us)
Async XLA Ops:
  1.9 1.0 copy-start.2
  3.0 0.7 copy-start.1
  160.0 1.4 copy-start

commit v4 on v3

--- a/solution.py
+++ b/solution.py
@@ -1,3 +1,5 @@
+import math
+
 import jax
 import jax.numpy as jnp
 from jax import lax
@@ -13,6 +15,7 @@
 SPAN = 528
 KEYS = 2 * SPAN
 CHUNKS = 4
+TEMPER = 128 ** (-0.5) * math.log2(math.e)
 MASKED = -1e30
 FLOOR = -1e29
 EPS = 1e-06
@@ -85,13 +88,12 @@
     gs, gr, us, ur, ds_, dr, gus, gur, hds, hdr, pas, par, bs, br, es, er, ls,
 ):
     r, s, x, y = place()
-    h = rem(x, 2)
     b = rem(y, 2)
+    h = b
     j = div(y, 2)
     top = div(y, 4)
     mate = s + NX - 2 * NX * b
-    twin = s + 1 - 2 * h
-    number = y * 2 + div(x, 2)
+    number = div(y, 2) * NX + x
     barrier = pltpu.get_barrier_semaphore()
 
     @loop(NS, 1)
@@ -125,27 +127,26 @@
     own_u.start()
     own_d.start()
 
+    mine_q = lanes(h * 2048, 2048)
+
     def qy_copy(d):
-        return remote(q, qy.at[y], qys.at[d], qyr.at[d], r, rem(y + spread_of(d, NY), NY) * NX + x)
+        to = rem(y + spread_of(d, NY), NY)
+        return remote(q.at[:, lanes(rem(to, 2) * 2048, 2048)], qy.at[y], qys.at[d], qyr.at[d], r, to * NX + x)
 
     def qx_copy(d, e):
         row = rem(y + NY - spread_of(d, NY), NY)
-        to = x_at(e)
-        cols = lanes(rem(to, 2) * 2048, 2048)
-        return remote(qy.at[row, :, cols], q_got.at[row * NX + x], qxs.at[d, e], qxr.at[d, e], r, y * NX + to)
+        return remote(qy.at[row], q_got.at[row * NX + x], qxs.at[d, e], qxr.at[d, e], r, y * NX + x_at(e))
 
     def first_copy(e):
-        to = x_at(e)
-        cols = lanes(rem(to, 2) * 2048, 2048)
-        return remote(q.at[:, cols], q_got.at[y * NX + x], qxs.at[NY - 1, e], qxr.at[NY - 1, e], r, y * NX + to)
+        return remote(q.at[:, mine_q], q_got.at[s], qxs.at[NY - 1, e], qxr.at[NY - 1, e], r, y * NX + x_at(e))
 
     def kv_copies():
         ctx, new = pl.ds(0, 512), pl.ds(512, 16)
         return (
-            remote(kv_in.at[1 - h], k.at[h, ctx], ks.at[0], kr.at[0], r, twin),
-            remote(kv_in.at[3 - h], v.at[h, ctx], ks.at[1], kr.at[1], r, twin),
-            remote(tree_in.at[1 - h], k.at[h, new], ks.at[2], kr.at[2], r, twin),
-            remote(tree_in.at[3 - h], v.at[h, new], ks.at[3], kr.at[3], r, twin),
+            remote(kv_in.at[1 - h], k.at[h, ctx], ks.at[0], kr.at[0], r, mate),
+            remote(kv_in.at[3 - h], v.at[h, ctx], ks.at[1], kr.at[1], r, mate),
+            remote(tree_in.at[1 - h], k.at[h, new], ks.at[2], kr.at[2], r, mate),
+            remote(tree_in.at[3 - h], v.at[h, new], ks.at[3], kr.at[3], r, mate),
         )
 
     def column(to):
@@ -165,7 +166,6 @@
         first_copy(e).start()
     for copy in kv_copies():
         copy.start()
-    mine_q = lanes(h * 2048, 2048)
     q_got[s] = q[:, mine_q]
     k[h, 0:512] = kv_in[h]
     k[h, 512:528] = tree_in[h]
@@ -184,7 +184,7 @@
         for e in (2, 1, 3):
             qx_copy(d, e).start()
         row = rem(y + NY - spread_of(d, NY), NY)
-        q_got[row * NX + x] = qy[row, :, mine_q]
+        q_got[row * NX + x] = qy[row]
 
     @loop(NS - 1)
     def _(d):
@@ -199,13 +199,14 @@
         reach[...] = jnp.minimum(dot(reach[...], reach[...]), 1.0).astype(BF)
 
     reach_f[...] = jnp.where(reach[...].astype(F32) > 0.5, 0.0, MASKED)
-    kin = reach_f[pl.ds(pl.multiple_of(8 * div(s, 2), 8), 8), :]
+    base = s - NX * h
     spot = lax.broadcasted_iota(jnp.int32, (SPAN, 128), 0)
     for p in range(2):
-        first = (s - h + p) * 512
+        first = (base + NX * p) * 512
+        eight = reach_f[pl.ds(pl.multiple_of(8 * (div(base, 2) + 2 * p), 8), 8), :]
         seen = (spot < 512) & (spot + first < length[0])
         bias[p * SPAN : (p + 1) * SPAN, :] = jnp.where(seen, 0.0, MASKED)
-        bias[p * SPAN + 512 : p * SPAN + 516, :] = kin[4 * p : 4 * p + 4, :]
+        bias[p * SPAN + 512 : p * SPAN + 516, :] = jnp.where(rem(base, 2) == 1, eight[4:8, :], eight[0:4, :])
 
     earlier = lax.broadcasted_iota(jnp.int32, (128, 128), 0) < lax.broadcasted_iota(jnp.int32, (128, 128), 1)
     slot = dot(chosen[...].astype(BF), jnp.where(earlier, 1.0, 0.0).astype(BF))
@@ -264,9 +265,9 @@
         score = lax.dot_general(
             k[...].reshape(KEYS, 128), heads, (((1,), (1,)), ((), ())), preferred_element_type=F32
         )
-        score = score * (128 ** (-0.5)) + bias[...]
+        score = score + bias[...]
         peak = jnp.maximum(jnp.max(score, axis=0, keepdims=True), FLOOR)
-        prob = jnp.exp(score - peak)
+        prob = jnp.exp2((score - peak) * TEMPER)
         total = jnp.sum(prob, axis=0, keepdims=True)
         prob = prob.astype(BF)
         out_src[i] = (dot(vt[0], prob[:SPAN]) + dot(vt[1], prob[SPAN:])).astype(BF)
@@ -291,7 +292,7 @@
 
     @loop(16)
     def _(n):
-        who = div(n, 2) * NX + 2 * rem(n, 2) + top
+        who = (2 * div(n, NX) + top) * NX + rem(n, NX)
 
         @pl.when(who != s)
         def _():
@@ -301,7 +302,7 @@
     peaks = got_st[:, 0:1, :]
     totals = got_st[:, 1:2, :]
     peak = jnp.max(peaks, axis=0)
-    factor = jnp.exp(peaks - peak[None])
+    factor = jnp.exp2((peaks - peak[None]) * TEMPER)
     denom = jnp.sum(factor * totals, axis=0)
     numer = jnp.zeros((128, 128), F32)
     for n in range(16):
@@ -312,17 +313,13 @@
         t = rem(y + FAR[n], NY)
         return remote(p_src.at[e, t], p_got.at[e, t], ps.at[e, n], pr.at[e, n], r, y * NX + x_at(e))
 
+    for e in (2, 1, 3, 0):
+        block = dot(att, w_out[:, lanes(x_at(jnp.int32(e)) * 1024, 1024)]).astype(BF)
+        for t in range(NY):
+            p_src[e, t] = block[:, part_of(t)]
     for n in range(NY):
-        t = rem(y + FAR[n], NY)
-        for e in (2, 1, 3, 0):
-            cols = lanes(x_at(jnp.int32(e)) * 1024 + t * 128, 128)
-            p_src[e, t] = dot(att, w_out[:, cols]).astype(BF)
-            if e:
-                p_copy(e, n).start()
-    for e in (2, 1, 3):
-        up_copy(jnp.int32(e)).start()
-    for e in (2, 1, 3):
-        down_copy(jnp.int32(e)).start()
+        for e in (2, 1, 3):
+            p_copy(e, n).start()
 
     def y_copy(n):
         to = rem(y + FAR[n], NY)
@@ -382,6 +379,11 @@
     def _(d):
         a_copy(d).start()
 
+    for e in (2, 1, 3):
+        up_copy(jnp.int32(e)).start()
+    for e in (2, 1, 3):
+        down_copy(jnp.int32(e)).start()
+
     @loop(4)
     def _(t):
         @pl.when(4 * b + t != y)
@@ -620,7 +622,7 @@
         in_specs=[VM] * 5 + [pl.BlockSpec(memory_space=pltpu.SMEM)] + [VM] * 4 + [HB] * 3,
         out_specs=(VM, VM),
         scratch_shapes=[
-            vm(NY, 4, 4096), vm(NS, 4, 2048), vm(128, 2048, dtype=F32), vm(2, SPAN, 128), vm(2, SPAN, 128), vm(2, 128, SPAN),
+            vm(NY, 4, 2048), vm(NS, 4, 2048), vm(128, 2048, dtype=F32), vm(2, SPAN, 128), vm(2, SPAN, 128), vm(2, 128, SPAN),
             vm(KEYS, 128, dtype=F32), vm(NS, 4, 128), vm(128, 128, dtype=F32), vm(128, 128),
             vm(128, 128, dtype=F32), vm(NR, 128, dtype=F32), vm(NR, 128, dtype=F32), vm(512, 128), vm(128, 512),
             vm(16, 128, 128), vm(16, 2, 128, dtype=F32), vm(16, 128, 128), vm(16, 2, 128, dtype=F32),

time: 162 us -> 140 us (0.86)
  Pallas kernels: 155 us -> 133 us
    pallas_call x1, Pallas kernels: 155 us -> 133 us  [body(): pl.pallas_call(layer_kernel, name='layer', out_shape=(sds((4, 4096)), sds...]
where the time goes in v4:
time: 140 us
  Pallas kernels  133 us (95%)
  local copies, waits for them, and re-layouts  5.65 us (4%)
    pallas_call x1, Pallas kernels, body(): pl.pallas_call(layer_kernel, name='layer', out_shape=(sds((4, 4096)), sds...  133 us
    unnamed x9, local copies, waits for them, and re-layouts  3.41 us

profile of v4, /device:TPU:1, one launch (start us, length us, event | category | flops | bytes accessed | tf_op | source)
XLA Modules:
  0.0 139.8 jit_solution(17923081910406334602)
XLA Ops:
  0.6 1.3 copy.15
  1.9 0.0 copy-start.2
  2.0 1.0 copy.16
  3.0 0.0 copy-done.2
  3.0 0.0 copy-start.1
  3.0 0.6 pad.4.tree_in
  3.6 0.1 copy-done.1
  3.7 0.6 reshape.7.gain
  4.9 132.8 %layer.1 = (bf16[4,4096]{1,0:T(4,128)(2,1)}, bf16[4,4096]{1,0:T(4,128)(2,1)}) custom-call(bf16[4,4096]{1,0:T(4,128)(2,1)} %bitcast.23, bf16[4,512,128]{2,1,0:T(8,128)(2,1)} %bitcast.19, bf16[4,16,128]{2,1,0:T(8,128)(2,1)} %pad.4.tree_in, bf16[4,4096]{1,0:T(4,128)(2,1)} %bitcast.24, s32[1,128]{1,0:T(1,128)} %parents.1, s32[1]{0:T(128)S(6)} %copy.22.length, ...), custom_call_target="tpu_custom_call" | custom-call | tf_op jit(solution)/shard_map/layer/pallas_call | solution.py:618
  137.7 0.0 copy-start
  137.8 1.4 copy.23
  139.1 0.0 copy-done
  139.1 0.6 copy.24
  (2 shorter events, 0.0 us)
Async XLA Ops:
  1.9 1.0 copy-start.2
  3.0 0.7 copy-start.1
  137.7 1.4 %copy-start = (bf16[4,4096]{1,0:T(4,128)(2,1)S(1)}, bf16[4,4096]{1,0:T(4,128)(2,1)}, u32[]{:S(2)}) copy-start(bf16[4,4096]{1,0:T(4,128)(2,1)} %get-tuple-element.5) | copy-start | bytes 98308

commit v5 on v4

--- a/solution.py
+++ b/solution.py
@@ -15,6 +15,10 @@
 SPAN = 528
 KEYS = 2 * SPAN
 CHUNKS = 4
+ASKS = NR // CHUNKS
+SEATS = 32 * ASKS
+STEPS = "FFFGFGGHGHDHDRHDRDRR"
+CHUNK_OF = "01203120310210321323"
 TEMPER = 128 ** (-0.5) * math.log2(math.e)
 MASKED = -1e30
 FLOOR = -1e29
@@ -63,7 +67,7 @@
 
 
 def reach_of(o):
-    return spread_of(o, NR)
+    return jnp.where(o < 4, spread_of(NR - 1 - o, NR), spread_of(o - 4, NR))
 
 
 FAR = (4, 3, 5, 2, 6, 1, 7, 0)
@@ -75,12 +79,20 @@
 
 def part_of(g):
     return slice(128 * g, 128 * g + 128)
+
+
+def seats_of(g):
+    return slice(SEATS * g, SEATS * g + SEATS)
+
+
+def asks_of(g):
+    return range(max(ASKS * g, 1), ASKS * g + ASKS)
 
 
 def layer_kernel(
     q, kv_in, tree_in, res, parents, length, ids, gates, gain, w_out, w_gate, w_up, w_down,
     a_out, e_out,
-    qy, q_got, qf, k, v, vt, bias, res_got, rf, reach, reach_f, chosen, rates, sel, back,
+    qy, q_got, qf, kt, k, v, vt, bias, res_got, rf, reach, reach_f, chosen, rates, sel, back,
     out_src, st_src, got, got_st, p_src, p_got, y_src, y_got, a_src, sq_src, sq, mid_src, mid_q,
     d_src, rows, wgu, wd, gu_src, gu, hid_src, hid, pair_src, pair, ret_src, ret, f_src, fin,
     qys, qyr, qxs, qxr, ks, kr, rs, rr,
@@ -143,10 +155,10 @@
     def kv_copies():
         ctx, new = pl.ds(0, 512), pl.ds(512, 16)
         return (
-            remote(kv_in.at[1 - h], k.at[h, ctx], ks.at[0], kr.at[0], r, mate),
-            remote(kv_in.at[3 - h], v.at[h, ctx], ks.at[1], kr.at[1], r, mate),
+            remote(kv_in.at[1 - h], kt.at[h], ks.at[0], kr.at[0], r, mate),
+            remote(kv_in.at[3 - h], vt.at[h, :, ctx], ks.at[1], kr.at[1], r, mate),
             remote(tree_in.at[1 - h], k.at[h, new], ks.at[2], kr.at[2], r, mate),
-            remote(tree_in.at[3 - h], v.at[h, new], ks.at[3], kr.at[3], r, mate),
+            remote(tree_in.at[3 - h], v.at[h], ks.at[3], kr.at[3], r, mate),
         )
 
     def column(to):
@@ -167,10 +179,10 @@
     for copy in kv_copies():
         copy.start()
     q_got[s] = q[:, mine_q]
-    k[h, 0:512] = kv_in[h]
+    kt[h] = kv_in[h]
     k[h, 512:528] = tree_in[h]
-    v[h, 0:512] = kv_in[2 + h]
-    v[h, 512:528] = tree_in[2 + h]
+    vt[h, :, 0:512] = kv_in[2 + h]
+    v[h] = tree_in[2 + h]
     res_got[s] = res[:, column(s)]
 
     for o in range(NR):
@@ -211,7 +223,7 @@
     earlier = lax.broadcasted_iota(jnp.int32, (128, 128), 0) < lax.broadcasted_iota(jnp.int32, (128, 128), 1)
     slot = dot(chosen[...].astype(BF), jnp.where(earlier, 1.0, 0.0).astype(BF))
     seat = lax.broadcasted_iota(jnp.int32, (32, 128), 0).astype(F32)
-    for g in range(CHUNKS):
+    for g in range(4):
         tall = []
         for o in range(4 * g, 4 * g + 4):
             hit = (slot[o : o + 1, :] == seat) & (chosen[o : o + 1, :] > 0.5)
@@ -223,8 +235,8 @@
         copy.wait()
     for p in range(2):
         for t in range(4):
-            vt[p, :, part_of(t)] = jnp.transpose(v[p, part_of(t), :].astype(F32)).astype(BF)
-        last = jnp.concatenate([v[p, 512:528, :].astype(F32), jnp.zeros((112, 128), F32)], axis=0)
+            k[p, part_of(t), :] = jnp.transpose(kt[p, :, part_of(t)].astype(F32)).astype(BF)
+        last = jnp.concatenate([v[p].astype(F32), jnp.zeros((112, 128), F32)], axis=0)
         vt[p, :, 512:528] = jnp.transpose(last)[:, 0:16].astype(BF)
     for e in range(1, NX):
         first_copy(e).wait()
@@ -244,8 +256,8 @@
     def st_copy(i):
         return remote(st_src.at[i], got_st.at[number], ts.at[i], tr.at[number], r, 16 * h + i)
 
-    def head_at(n):
-        return rem(n + number, 16)
+    def pair_at(n):
+        return rem(n + div(number, 2), 8)
 
     def send_head(i):
         @pl.when(16 * h + i != s)
@@ -258,29 +270,35 @@
             got[number] = out_src[i]
             got_st[number] = st_src[i]
 
-    @loop(16)
+    @loop(8)
     def _(n):
-        i = head_at(n)
-        heads = qf[:, lanes(i * 128, 128)].astype(BF)
+        p = pair_at(n)
+        two = qf[:, lanes(p * 256, 256)].astype(BF)
+        heads = jnp.concatenate([two[:, 0:128], two[:, 128:256]], axis=0)
         score = lax.dot_general(
             k[...].reshape(KEYS, 128), heads, (((1,), (1,)), ((), ())), preferred_element_type=F32
         )
-        score = score + bias[...]
+        mask = bias[...]
+        score = jnp.concatenate([score[:, 0:128] + mask, score[:, 128:256] + mask], axis=1)
         peak = jnp.maximum(jnp.max(score, axis=0, keepdims=True), FLOOR)
         prob = jnp.exp2((score - peak) * TEMPER)
         total = jnp.sum(prob, axis=0, keepdims=True)
         prob = prob.astype(BF)
-        out_src[i] = (dot(vt[0], prob[:SPAN]) + dot(vt[1], prob[SPAN:])).astype(BF)
-        st_src[i] = jnp.concatenate([peak, total], axis=0)
+        out = (dot(vt[0], prob[:SPAN]) + dot(vt[1], prob[SPAN:])).astype(BF)
+        for t in range(2):
+            out_src[2 * p + t] = out[:, part_of(t)]
+            st_src[2 * p + t] = jnp.concatenate([peak[:, part_of(t)], total[:, part_of(t)]], axis=0)
 
         @pl.when(n >= 1)
         def _():
-            send_head(head_at(n + 15))
+            send_head(2 * pair_at(n + 7))
+            send_head(2 * pair_at(n + 7) + 1)
 
         for e in (1, 3):
-            gate_copy(jnp.int32(e), pl.multiple_of(64 * n, 64), 64).start()
-
-    send_head(head_at(jnp.int32(15)))
+            gate_copy(jnp.int32(e), pl.multiple_of(128 * n, 128), 128).start()
+
+    send_head(2 * pair_at(jnp.int32(7)))
+    send_head(2 * pair_at(jnp.int32(7)) + 1)
     gate_copy(jnp.int32(2)).start()
 
     @loop(NS - 1)
@@ -320,6 +338,7 @@
     for n in range(NY):
         for e in (2, 1, 3):
             p_copy(e, n).start()
+    up_copy(jnp.int32(2)).start()
 
     def y_copy(n):
         to = rem(y + FAR[n], NY)
@@ -379,7 +398,7 @@
     def _(d):
         a_copy(d).start()
 
-    for e in (2, 1, 3):
+    for e in (1, 3):
         up_copy(jnp.int32(e)).start()
     for e in (2, 1, 3):
         down_copy(jnp.int32(e)).start()
@@ -415,27 +434,28 @@
             for t in range(4)
         ], axis=1
     )
-    for g in range(CHUNKS):
+    for g in range(4):
         d_src[4 * g : 4 * g + 4] = dot(sel[part_of(g), :], normed).astype(BF).reshape(4, 32, 512)
-        for o in range(4 * g, min(4 * g + 4, NR - 1)):
+        if g == 0:
+            rows[b, 0] = d_src[0]
+            pass_copy(jnp.int32(0)).start()
+        for o in range(max(4 * g, 1), 4 * g + 4):
             z_copy(jnp.int32(o)).start()
-    rows[b, NR - 1] = d_src[NR - 1]
-    pass_copy(jnp.int32(NR - 1)).start()
 
     def gu_copy(e, g):
         return remote(
-            gu_src.at[e, pl.ds(128 * g, 128)], gu.at[e, pl.ds(128 * g, 128)], gus.at[e, g], gur.at[e, g],
+            gu_src.at[e, pl.ds(SEATS * g, SEATS)], gu.at[e, pl.ds(SEATS * g, SEATS)], gus.at[e, g], gur.at[e, g],
             r, y * NX + x_at(e),
         )
 
     def hid_copy(e, g):
         return remote(
-            hid_src.at[pl.ds(128 * g, 128)], hid.at[x, pl.ds(128 * g, 128)], hds.at[e, g], hdr.at[e, g],
+            hid_src.at[pl.ds(SEATS * g, SEATS)], hid.at[x, pl.ds(SEATS * g, SEATS)], hds.at[e, g], hdr.at[e, g],
             r, y * NX + x_at(e),
         )
 
     def pair_copy(g):
-        span = pl.ds(128 * g, 128)
+        span = pl.ds(SEATS * g, SEATS)
         return remote(pair_src.at[span], pair.at[span], pas.at[g], par.at[g], r, mate)
 
     def b_copy(o):
@@ -443,7 +463,7 @@
         return remote(ret_src.at[o], ret.at[o], bs.at[o], br.at[o], to, s)
 
     def forward(g):
-        for o in range(4 * g, min(4 * g + 4, NR - 1)):
+        for o in asks_of(g):
             z_copy(jnp.int32(o)).wait_recv()
             pass_copy(jnp.int32(o)).start()
 
@@ -454,32 +474,32 @@
             for e in range(1, NX):
                 gate_copy(jnp.int32(e)).wait()
                 up_copy(jnp.int32(e)).wait()
-        for o in range(4 * g, 4 * g + 4):
+        for o in range(ASKS * g, ASKS * g + ASKS):
             pass_got(jnp.int32(o)).wait_recv()
-        left = rows[0, 4 * g : 4 * g + 4].reshape(128, 512)
-        right = rows[1, 4 * g : 4 * g + 4].reshape(128, 512)
+        left = rows[0, ASKS * g : ASKS * g + ASKS].reshape(SEATS, 512)
+        right = rows[1, ASKS * g : ASKS * g + ASKS].reshape(SEATS, 512)
         for e in (2, 1, 3, 0):
             to = x_at(jnp.int32(e))
-            gu_src[e, part_of(g), :] = (dot(left, wgu[to, 0:512, :]) + dot(right, wgu[to, 512:1024, :])).astype(BF)
+            gu_src[e, seats_of(g), :] = (dot(left, wgu[to, 0:512, :]) + dot(right, wgu[to, 512:1024, :])).astype(BF)
             if e:
                 gu_copy(e, g).start()
 
     def hidden(g):
-        acc = gu_src[0, part_of(g), :].astype(F32)
+        acc = gu_src[0, seats_of(g), :].astype(F32)
         for e in range(1, NX):
             gu_copy(e, g).wait_recv()
-            acc = acc + gu[e, part_of(g), :].astype(F32)
+            acc = acc + gu[e, seats_of(g), :].astype(F32)
         gate = acc[:, 0:128]
-        hid_src[part_of(g), :] = (gate / (1.0 + jnp.exp(-gate)) * acc[:, 128:256]).astype(BF)
+        hid_src[seats_of(g), :] = (gate / (1.0 + jnp.exp(-gate)) * acc[:, 128:256]).astype(BF)
         for e in (2, 1, 3):
             hid_copy(e, g).start()
-        hid[x, part_of(g), :] = hid_src[part_of(g), :]
+        hid[x, seats_of(g), :] = hid_src[seats_of(g), :]
 
     def product(g, side):
         cols = lanes(side * 512, 512)
-        acc = dot(hid[0, part_of(g), :], wd[0, :, cols])
+        acc = dot(hid[0, seats_of(g), :], wd[0, :, cols])
         for t in range(1, NX):
-            acc = acc + dot(hid[t, part_of(g), :], wd[t, :, cols])
+            acc = acc + dot(hid[t, seats_of(g), :], wd[t, :, cols])
         return acc
 
     def down(g):
@@ -489,43 +509,26 @@
                 down_copy(jnp.int32(e)).wait()
         for e in range(1, NX):
             hid_copy(e, g).wait_recv()
-        pair_src[part_of(g), :] = product(g, 1 - b).astype(BF)
+        pair_src[seats_of(g), :] = product(g, 1 - b).astype(BF)
         pair_copy(g).start()
 
     def give(g):
         acc = product(g, b)
         pair_copy(g).wait_recv()
-        acc = acc + pair[part_of(g), :].astype(F32)
-        ret_src[4 * g : 4 * g + 4] = acc.astype(BF).reshape(4, 32, 512)
-        for o in range(4 * g, min(4 * g + 4, NR - 1)):
+        acc = acc + pair[seats_of(g), :].astype(F32)
+        ret_src[ASKS * g : ASKS * g + ASKS] = acc.astype(BF).reshape(ASKS, 32, 512)
+        for o in asks_of(g):
             b_copy(jnp.int32(o)).start()
-        if g == CHUNKS - 1:
-            ret[NR - 1] = ret_src[NR - 1]
-
-    forward(0)
-    forward(1)
-    gate_up(0)
-    forward(2)
-    gate_up(1)
-    forward(3)
-    gate_up(2)
-    hidden(0)
-    gate_up(3)
-    hidden(1)
-    down(0)
-    hidden(2)
-    down(1)
-    give(0)
-    hidden(3)
-    down(2)
-    give(1)
-    down(3)
-    give(2)
-    give(3)
+        if g == 0:
+            ret[0] = ret_src[0]
+
+    steps = {"F": forward, "G": gate_up, "H": hidden, "D": down, "R": give}
+    for name, g in zip(STEPS, CHUNK_OF):
+        steps[name](int(g))
 
     total = jnp.zeros((128, 512), F32)
-    for g in range(CHUNKS):
-        for o in range(4 * g, min(4 * g + 4, NR - 1)):
+    for g in range(4):
+        for o in range(max(4 * g, 1), 4 * g + 4):
             b_copy(jnp.int32(o)).wait_recv()
         total = total + dot(back[:, part_of(g)], ret[4 * g : 4 * g + 4].reshape(128, 512))
     for t in range(NS):
@@ -569,7 +572,7 @@
         sq_copy(d).wait_send()
         a_copy(d).wait()
 
-    @loop(NR - 1)
+    @loop(NR, 1)
     def _(o):
         z_copy(o).wait_send()
         b_copy(o).wait_send()
@@ -613,7 +616,7 @@
     queries, kv_cache, tree_kv, context_lengths, tree_parents, resid, out_weight, norm_gain,
     expert_ids, gate_weights, w_gate, w_up, w_down,
 ):
-    kv_in = kv_cache[0].reshape(512, 4, 128).transpose(1, 0, 2)
+    kv_in = kv_cache[0].reshape(512, 4, 128).transpose(1, 2, 0)
     tree_in = jnp.pad(tree_kv[0].reshape(4, 4, 128).transpose(1, 0, 2), ((0, 0), (0, 12), (0, 0)))
     a_out, e_out = pl.pallas_call(
         layer_kernel,
@@ -622,7 +625,7 @@
         in_specs=[VM] * 5 + [pl.BlockSpec(memory_space=pltpu.SMEM)] + [VM] * 4 + [HB] * 3,
         out_specs=(VM, VM),
         scratch_shapes=[
-            vm(NY, 4, 2048), vm(NS, 4, 2048), vm(128, 2048, dtype=F32), vm(2, SPAN, 128), vm(2, SPAN, 128), vm(2, 128, SPAN),
+            vm(NY, 4, 2048), vm(NS, 4, 2048), vm(128, 2048, dtype=F32), vm(2, 128, 512), vm(2, SPAN, 128), vm(2, 16, 128), vm(2, 128, SPAN),
             vm(KEYS, 128, dtype=F32), vm(NS, 4, 128), vm(128, 128, dtype=F32), vm(128, 128),
             vm(128, 128, dtype=F32), vm(NR, 128, dtype=F32), vm(NR, 128, dtype=F32), vm(512, 128), vm(128, 512),
             vm(16, 128, 128), vm(16, 2, 128, dtype=F32), vm(16, 128, 128), vm(16, 2, 128, dtype=F32),

time: 140 us -> 141 us (level)
  no operation moved by 1% of the time
where the time goes in v5:
time: 141 us; the launch traced here: 140 us
  Pallas kernels  133 us (94%)
  local copies, waits for them, and re-layouts  6.01 us (4%)
    pallas_call x1, Pallas kernels, body(): pl.pallas_call(layer_kernel, name='layer', out_shape=(sds((4, 4096)), sds...  133 us
    unnamed x9, local copies, waits for them, and re-layouts  4.77 us

profile of v5, /device:TPU:1, one launch (start us, length us, event | category | flops | bytes accessed | tf_op | source)
XLA Modules:
  0.0 140.2 jit_solution(3297457618932233708)
XLA Ops:
  1.3 0.0 copy-start.2
  1.3 0.7 copy-done.2
  2.0 0.0 copy-start.1
  2.0 0.6 pad.4.tree_in
  2.6 0.1 copy-done.1
  2.7 0.6 reshape.7.gain
  3.3 2.0 %copy.16 = bf16[1,512,2,256]{1,3,2,0:T(8,128)(2,1)} copy(bf16[1,512,2,256]{3,2,1,0:T(2,128)(2,1)} %param.14) | data formatting | bytes 1048576 | tf_op args[1]
  5.3 132.9 %layer.1 = (bf16[4,4096]{1,0:T(4,128)(2,1)}, bf16[4,4096]{1,0:T(4,128)(2,1)}) custom-call(bf16[4,4096]{1,0:T(4,128)(2,1)} %bitcast.23, bf16[4,128,512]{2,1,0:T(8,128)(2,1)} %bitcast.19, bf16[4,16,128]{2,1,0:T(8,128)(2,1)} %pad.4.tree_in, bf16[4,4096]{1,0:T(4,128)(2,1)} %bitcast.24, s32[1,128]{1,0:T(1,128)} %parents.1, s32[1]{0:T(128)S(6)} %copy.22.length, ...), custom_call_target="tpu_custom_call" | custom-call | tf_op jit(solution)/shard_map/layer/pallas_call | solution.py:621
  138.2 0.0 copy-start
  138.2 1.4 copy.23
  139.6 0.0 copy-done
  139.6 0.6 copy.24
  (2 shorter events, 0.0 us)
Async XLA Ops:
  1.3 0.7 copy-start.2
  2.0 0.7 copy-start.1
  138.2 1.4 %copy-start = (bf16[4,4096]{1,0:T(4,128)(2,1)S(1)}, bf16[4,4096]{1,0:T(4,128)(2,1)}, u32[]{:S(2)}) copy-start(bf16[4,4096]{1,0:T(4,128)(2,1)} %get-tuple-element.5) | copy-start | bytes 98308
